TPU v7x, 256 devices: a whole 4x4x8 slice. The times are simulated.
256 devices in a mesh: dp: 4 (over x_lo, core), expert: 64 (over x_hi, y, z).
Axes of the slice: x: 4 (x_hi: 2, x_lo: 2; x = x_hi * 2 + x_lo), y: 4, z: 8, core: 2. Of those that a mesh axis runs over, the one named last changes fastest.
Arguments:
- tokens: bfloat16 [16384, 4096], P(('dp', 'expert')), may hold values from -6 to 6
- token_experts: int32 [16384, 8], P(('dp', 'expert')), may hold values from 0 to 63, all different within a row; in each aligned block of 64 rows (0 to 63, 64 to 127, ...) at most 12 rows name the same one
- hidden_grad: bfloat16 [16384, 8, 768], P(('dp', 'expert')), may hold values from -6 to 6
- held_expert: int32 [64], replicated, may hold values from 0 to 63, each once
- swap_mask: int32 [64], replicated, may hold values from 0 to 1, as said below
- weight: bfloat16 [64, 4096, 768], P('expert', 'dp'), may hold values from -0.09375 to 0.09375
- first_moment: float32 [64, 4096, 768], P('expert', 'dp'), may hold values from -81.4587 to 81.4587
- second_moment: float32 [64, 4096, 768], P('expert', 'dp'), may hold values from 20.48 to 204.8
Outputs:
- token_grad: bfloat16 [16384, 4096], P(('dp', 'expert'))
- adam_step: bfloat16 [64, 4096, 768], P('expert', 'dp')
Inputs may be any that keep to these rules, and one draw needn't show every extreme that they name: `token_experts`: in each aligned block of 64 rows (the tokens of one device) no expert is named by more than 12 rows, and in some blocks one is named by exactly 12; the ids of a row differ. `held_expert`: a permutation of the expert ids. swap_mask[p] equals swap_mask[p + 32] for p below 32, and exactly 8 such pairs are 1.
All inputs are finite; a program needn't handle non-finite values.
Results may differ from a plain program's by a relative error of at most 0.008.
Values may be sent and summed in bfloat16 or wider, within the bound.
No kernel may reach another device: no remote copies, remote signals or barrier semaphores. Data moves between devices by JAX's collectives and lax.ppermute only.
A program may use at most 128 MiB of HBM per device.

v0:
```python
import functools

import jax
import jax.numpy as jnp
import numpy as np
from jax import lax
from jax.experimental import pallas as pl
from jax.experimental.pallas import tpu as pltpu
from jax.sharding import Mesh, PartitionSpec as P

CAP = 12
PLANES = 8
LANES = 8
GROUPS = ((-1, 1), (3, 0, 2, -2), (-4, -3))
BACK = ((1, 0), (2, 0), (1, 1), (0, 0))
SWAP_PARTS = 2


def adam_kernel(a, b, c, first, second, out):
    grad = a[...].astype(jnp.float32) + b[...].astype(jnp.float32) + c[...].astype(jnp.float32)
    first_new = 0.9 * first[0] + 0.1 * grad
    second_new = 0.95 * second[0] + 0.05 * grad * grad
    out[...] = (first_new / (jnp.sqrt(second_new) + 1e-08)).astype(out.dtype)


def adam_direction(own, from_core, from_x, first, second, part):
    rows, hidden = from_x.shape
    bn = 64
    skip = part * (rows // bn)
    here = pl.BlockSpec((bn, hidden), lambda i: (i + skip, 0))
    short = pl.BlockSpec((bn, hidden), lambda i: (i, 0))
    moment = pl.BlockSpec((1, bn, hidden), lambda i: (0, i + skip, 0))
    return pl.pallas_call(
        adam_kernel,
        grid=(rows // bn,),
        in_specs=[here, here, short, moment, moment],
        out_specs=short,
        out_shape=jax.ShapeDtypeStruct((rows, hidden), jnp.bfloat16),
        cost_estimate=pl.CostEstimate(
            flops=12 * rows * hidden, bytes_accessed=16 * rows * hidden, transcendentals=0
        ),
        name="adam",
    )(own, from_core, from_x, first, second)


def dot(a, b, contract=((1,), (0,))):
    return lax.dot_general(a, b, (contract, ((), ())), preferred_element_type=jnp.float32)


def exchange_plane(block):
    groups = [
        [((low ^ high) * 2 + high) * 4 + y for high in range(2) for y in range(4)]
        for low in range(2)
    ]
    return lax.all_to_all(block, ("xl", "xh", "y"), 0, 0, axis_index_groups=groups, tiled=True)


def swapped(block, axis):
    return lax.ppermute(block, axis, [(0, 1), (1, 0)])


def shifted(block, by):
    return lax.ppermute(block, "z", [(i, (i + by) % PLANES) for i in range(PLANES)])


def dw_kernel(count, me, *refs):
    xs, g, out, joined = refs[:count], refs[count], refs[count + 1], refs[count + 2]
    at = 0
    for x in xs:
        joined[pl.ds(at, x.shape[0]), :] = x[...]
        at += x.shape[0]
    out[...] = dot(joined[...], g[...], ((0,), (0,))).astype(out.dtype)


def weight_grad(me, xs, g, other):
    rows, hidden = g.shape
    width = xs[0].shape[1] - hidden
    shard = width // 4
    bn = 256
    per = shard // bn
    spec = [
        pl.BlockSpec((x.shape[0], bn), lambda i, m: (0, jnp.bitwise_xor(m[0], other) * per + i))
        for x in xs
    ]
    return pl.pallas_call(
        functools.partial(dw_kernel, len(xs)),
        grid_spec=pltpu.PrefetchScalarGridSpec(
            num_scalar_prefetch=1,
            grid=(per,),
            in_specs=spec + [pl.BlockSpec(g.shape, lambda i, m: (0, 0))],
            out_specs=pl.BlockSpec((bn, hidden), lambda i, m: (i, 0)),
            scratch_shapes=[pltpu.VMEM((rows, bn), jnp.bfloat16)],
        ),
        out_shape=jax.ShapeDtypeStruct((shard, hidden), jnp.bfloat16),
        cost_estimate=pl.CostEstimate(
            flops=2 * rows * shard * hidden,
            bytes_accessed=2 * (rows * shard + shard * hidden + g.size),
            transcendentals=0,
        ),
    )(me, *xs, g)


def pack_kernel(count, *refs):
    choose, wanted, wide, perm = refs[:4]
    cs, gs = refs[4 : 4 + count], refs[4 + count : 4 + 2 * count]
    sent, picks = refs[4 + 2 * count], refs[5 + 2 * count : -2]
    tokens, hidden = refs[-2:]
    for i, (c, g) in enumerate(zip(cs, gs)):
        tokens[pl.ds(i * c.shape[0], c.shape[0]), :] = c[...]
        hidden[pl.ds(i * g.shape[0], g.shape[0]), :] = g[...]
    width = sent.shape[1] - hidden.shape[1]
    value = dot(choose[...], tokens[:, width:], ((1,), (1,)))
    for i, pick in enumerate(picks):
        cols = pick.shape[1]
        part = value[:, i * cols : (i + 1) * cols]
        hit = (part[:, None, :] == wanted[...][None]).astype(jnp.float32)
        pick[...] = hit.reshape(pick.shape).astype(jnp.bfloat16)
    if count == 2:
        chosen = picks[0][...]
    else:
        hit = (value[:, None, :] == wide[...][None]).astype(jnp.float32)
        chosen = hit.reshape(perm.shape[0], value.shape[1]).astype(jnp.bfloat16)
    bn = 512

    def columns(i, carry):
        at = pl.ds(pl.multiple_of(i * bn, bn), bn)
        sent[:, at] = dot(chosen, tokens[:, at]).astype(sent.dtype)
        return carry

    lax.fori_loop(0, width // bn, columns, 0)
    sent[:, width:] = dot(perm[...], hidden[...]).astype(sent.dtype)


def wanted_rank(count, tok_dev):
    q, t = np.arange(count * CAP)[:, None], np.arange(count * tok_dev)[None, :]
    return jnp.asarray(np.where(q // CAP == t // tok_dev, q % CAP + 1.0, -1.0), jnp.float32)


def pack(choose, cs, gs, width):
    count, tok_dev, hidden = len(cs), cs[0].shape[0], gs[0].shape[1]
    rows = LANES * count * CAP
    order = [
        (s * LANES + j) * CAP + r for j in range(LANES) for s in range(count) for r in range(CAP)
    ]
    source = jnp.asarray(np.array(order, np.int32))[:, None]
    perm = (source == lax.broadcasted_iota(jnp.int32, (rows, rows), 1)).astype(jnp.bfloat16)
    pick = jax.ShapeDtypeStruct((LANES * 2 * CAP, 2 * tok_dev), jnp.bfloat16)
    return pl.pallas_call(
        functools.partial(pack_kernel, count),
        out_shape=[jax.ShapeDtypeStruct((rows, width + hidden), jnp.bfloat16)]
        + [pick] * (count // 2),
        scratch_shapes=[
            pltpu.VMEM((count * tok_dev, cs[0].shape[1]), jnp.bfloat16),
            pltpu.VMEM((rows, hidden), jnp.bfloat16),
        ],
    )(choose, wanted_rank(2, tok_dev), wanted_rank(count, tok_dev), perm, *cs, *gs)


def expert_kernel(steps, x, g0, g1, g2, w, grad, *rest):
    backs, acc = rest[:-1], rest[-1]
    phase, k = pl.program_id(0), pl.program_id(1)

    @pl.when(phase == 0)
    def _():
        part = dot(x[...], w[...])

        @pl.when(k == 0)
        def _():
            acc[...] = part

        @pl.when(k > 0)
        def _():
            acc[...] += part

        @pl.when(k == steps - 1)
        def _():
            wide = g0.shape[1]
            for i, g in enumerate((g0, g1, g2)):
                at = pl.ds(i * wide, wide)
                pre = acc[:, at]
                sig = jax.nn.sigmoid(pre)
                value = g[...].astype(jnp.float32) * sig * (1.0 + pre * (1.0 - sig))
                grad[:, at] = value.astype(grad.dtype)

    @pl.when(phase == 1)
    def _():
        value = dot(grad[...], w[...], ((1,), (1,)))
        rows, kb = value.shape
        split = value.reshape(LANES, rows // LANES, kb)
        for i, back in enumerate(backs):
            piece = split[:, i * 2 * CAP : (i + 1) * 2 * CAP]
            back[...] = piece.reshape(back.shape).astype(back.dtype)


def expert(got, full_w):
    width, hidden = full_w.shape
    rows = got.shape[0]
    kb = 1024
    nk = width // kb
    third = hidden // 3
    pair_rows = LANES * 2 * CAP
    pairs = rows // pair_rows
    side = [pl.BlockSpec((rows, third), lambda p, k, i=i: (0, width // third + i)) for i in range(3)]
    return pl.pallas_call(
        functools.partial(expert_kernel, nk),
        grid=(2, nk),
        in_specs=[pl.BlockSpec((rows, kb), lambda p, k: (0, jnp.where(p == 0, k, nk - 1)))]
        + side
        + [pl.BlockSpec((kb, hidden), lambda p, k: (k, 0))],
        out_specs=[pl.BlockSpec((rows, hidden), lambda p, k: (0, 0))]
        + [pl.BlockSpec((pair_rows, kb), lambda p, k: (0, jnp.where(p == 0, 0, k)))] * pairs,
        out_shape=[jax.ShapeDtypeStruct((rows, hidden), jnp.bfloat16)]
        + [jax.ShapeDtypeStruct((pair_rows, width), jnp.bfloat16)] * pairs,
        scratch_shapes=[pltpu.VMEM((rows, hidden), jnp.float32)],
        cost_estimate=pl.CostEstimate(
            flops=4 * rows * width * hidden,
            bytes_accessed=4 * width * (hidden + rows),
            transcendentals=rows * hidden,
        ),
    )(got, got, got, got, full_w)


def step(
    tokens, token_experts, hidden_grad, held_expert, swap_mask, weight, first_moment, second_moment
):
    bf16, f32, i32 = jnp.bfloat16, jnp.float32, jnp.int32
    xl, core, xh = lax.axis_index("xl"), lax.axis_index("core"), lax.axis_index("xh")
    y, z = lax.axis_index("y"), lax.axis_index("z")
    here = (xh * 4 + y) * PLANES + z
    me = xl * 2 + core
    tok_dev, top = token_experts.shape
    width, hidden = tokens.shape[1], hidden_grad.shape[2]
    slots = held_expert.shape[0]
    pair = 2 * CAP

    w_own = weight[0]
    w_x = swapped(w_own, "xl")
    w_c = swapped(jnp.stack([w_own, w_x]), "core")
    shard = w_own.shape[0]
    full_w = jnp.zeros((width, hidden), bf16)
    for i, piece in ((0, w_own), (2, w_x), (1, w_c[0]), (3, w_c[1])):
        full_w = lax.dynamic_update_slice(full_w, piece, ((me ^ i) * shard, 0))

    same = token_experts[:, :, None] == held_expert[None, None, :]
    named = jnp.sum(same.astype(f32), axis=1).astype(bf16)
    earlier = jnp.asarray(np.tril(np.ones((tok_dev, tok_dev)), -1), bf16)
    rank = named.astype(f32) * (dot(earlier, named) + 1.0)

    marks = jnp.pad(rank.astype(bf16), ((0, 0), (0, 128 - slots)))
    own = jnp.concatenate([tokens, marks], axis=1)
    column = {0: own}
    for k in range(1, 5):
        column[-k] = shifted(column[1 - k], 1)
        if k < 4:
            column[k] = shifted(column[k - 1], -1)

    slot_p = np.arange(slots)
    ahead = jnp.bitwise_and(jnp.asarray(slot_p % PLANES, i32) - z, PLANES - 1) * (LANES * CAP)
    place = (ahead + jnp.asarray(slot_p // PLANES * CAP - 1, i32)).astype(f32)
    slot = jnp.sum(jnp.where(same, (rank + place[None, :])[:, None, :], 0.0), axis=2)
    slot = slot.astype(i32).reshape(1, tok_dev * top)
    pick_g = (lax.broadcasted_iota(i32, (slots * CAP, tok_dev * top), 0) == slot).astype(bf16)
    send_g = dot(pick_g, hidden_grad.reshape(tok_dev * top, hidden)).astype(bf16)
    send_g = send_g.reshape(PLANES, LANES * CAP, hidden)
    grad_from = {0: send_g[0]}
    for d in (1, -1, 2, -2, 4, 3, -3):
        grad_from[-d] = shifted(send_g[d % PLANES], d)

    lane_i = lax.broadcasted_iota(i32, (LANES, 128), 0)
    slot_i = lax.broadcasted_iota(i32, (LANES, 128), 1)
    choose = (slot_i == lane_i * PLANES + z).astype(bf16)
    picks, xs, grads, backs = [], [], [], []
    for group in GROUPS:
        sent, *pick = pack(choose, [column[s] for s in group], [grad_from[s] for s in group], width)
        rows = sent.shape[0]
        got = exchange_plane(sent.reshape(LANES, rows // LANES, width + hidden))
        got = got.reshape(rows, width + hidden)
        grad, *back = expert(got, full_w)
        picks.append(pick)
        xs.append(got)
        grads.append(grad)
        backs.append(back)

    going = {}
    for n, h in BACK:
        back = exchange_plane(backs[n][h].reshape(LANES, pair, width))
        back = back.reshape(LANES * pair, width)
        for i, s in enumerate(GROUPS[n][2 * h : 2 * h + 2]):
            sign = 1 if s > 0 else -1
            part = dot(picks[n][h][:, i * tok_dev : (i + 1) * tok_dev], back, ((0,), (0,)))
            if s == 0:
                home = part
                continue
            if sign in going:
                part = part + going[sign].astype(f32)
            going[sign] = shifted(part.astype(bf16), sign)
    token_grad = (home + going[1].astype(f32) + going[-1].astype(f32)).astype(bf16)

    grad_rows = jnp.concatenate(grads, axis=0)
    me_ref = me.astype(i32).reshape(1)
    block = {}
    for other in (3, 2, 1, 0):
        block[other] = weight_grad(me_ref, xs, grad_rows, other)
    from_core_x = swapped(block[3], "core")
    from_core = swapped(block[1], "core")
    other = (block[2].astype(f32) + from_core_x.astype(f32)).astype(bf16)
    moving = jnp.sum(jnp.where(jnp.arange(slots, dtype=i32) == here, swap_mask, 0)) == 1
    size = shard // SWAP_PARTS
    steps = []
    for s in range(SWAP_PARTS):
        at = slice(s * size, (s + 1) * size)
        from_x = swapped(other[at], "xl")
        stepped = adam_direction(block[0], from_core, from_x, first_moment, second_moment, s)
        partner = swapped(stepped, "xh")
        steps.append(jnp.where(moving, partner, stepped))
    adam_step = jnp.concatenate(steps, axis=0)[None]
    return (token_grad, adam_step)


def solution(mesh):
    names = ("xl", "core", "xh", "y", "z")
    fine = Mesh(mesh.devices.reshape(2, 2, 2, 4, 8), names)
    dp, expert = ("xl", "core"), ("xh", "y", "z")
    in_specs = (
        P(names, None),
        P(names, None),
        P(names, None, None),
        P(),
        P(),
        P(expert, dp, None),
        P(expert, dp, None),
        P(expert, dp, None),
    )
    out_specs = (P(names, None), P(expert, dp, None))
    return jax.shard_map(step, mesh=fine, in_specs=in_specs, out_specs=out_specs, check_vma=False)
```

profile of v0, /device:TPU:120, one launch (start us, length us, event | category | flops | bytes accessed | tf_op | source)
XLA Modules:
  0.0 361.9 jit_solution(15584281644948303285)
XLA Ops:
  14.3 8.6 %collective-permute-done.10.refs_6_ = bf16[96,768]{1,0:T(8,128)(2,1)S(1)} collective-permute-done((bf16[96,768]{1,0:T(8,128)(2,1)S(1)}, bf16[96,768]{1,0:T(8,128)(2,1)S(1)}, u32[]{:S(2)}, u32[]{:S(2)}) %collective-permute-start.10) | collective-permute-done | bytes 147488 | tf_op jit(solution)/shard_map/ppermute | solution.py:63
  29.9 7.0 %all-to-all-start.2 = ((bf16[8,24,4864]{2,1,0:T(8,128)(2,1)}), bf16[8,24,4864]{2,1,0:T(8,128)(2,1)S(1)}, u32[]{:S(2)}, u32[]{:S(2)}) async-start(bf16[8,24,4864]{2,1,0:T(8,128)(2,1)} %bitcast.60), calls=%async_computation.2 | async-start | bytes 3735552 | tf_op jit(solution)/shard_map/all_to_all | solution.py:55
  40.0 10.1 %collective-permute-done.4.refs_7_ = bf16[64,4224]{1,0:T(8,128)(2,1)S(1)} collective-permute-done((bf16[64,4224]{1,0:T(8,128)(2,1)S(1)}, bf16[64,4224]{1,0:T(8,128)(2,1)S(1)}, u32[]{:S(2)}, u32[]{:S(2)}) %collective-permute-start.4) | collective-permute-done | bytes 540704 | tf_op jit(solution)/shard_map/ppermute | solution.py:63
  54.1 9.0 %collective-permute-done.15.refs_5_ = bf16[64,4224]{1,0:T(8,128)(2,1)S(1)} collective-permute-done((bf16[64,4224]{1,0:T(8,128)(2,1)S(1)}, bf16[64,4224]{1,0:T(8,128)(2,1)S(1)}, u32[]{:S(2)}, u32[]{:S(2)}) %collective-permute-start.15) | collective-permute-done | bytes 540704 | tf_op jit(solution)/shard_map/ppermute | solution.py:63
  70.5 6.5 %collective-permute-done.17.refs_6_ = bf16[96,768]{1,0:T(8,128)(2,1)S(1)} collective-permute-done((bf16[96,768]{1,0:T(8,128)(2,1)}, bf16[96,768]{1,0:T(8,128)(2,1)S(1)}, u32[]{:S(2)}, u32[]{:S(2)}) %collective-permute-start.17) | collective-permute-done | bytes 147488 | tf_op jit(solution)/shard_map/ppermute | solution.py:63
  77.0 14.1 %collective-permute-done.18.refs_7_ = bf16[96,768]{1,0:T(8,128)(2,1)S(1)} collective-permute-done((bf16[96,768]{1,0:T(8,128)(2,1)}, bf16[96,768]{1,0:T(8,128)(2,1)S(1)}, u32[]{:S(2)}, u32[]{:S(2)}) %collective-permute-start.18) | collective-permute-done | bytes 147488 | tf_op jit(solution)/shard_map/ppermute | solution.py:63
  98.5 6.9 %all-to-all-start.5 = ((bf16[8,24,4864]{2,1,0:T(8,128)(2,1)}), bf16[8,24,4864]{2,1,0:T(8,128)(2,1)}, u32[]{:S(2)}, u32[]{:S(2)}) async-start(bf16[8,24,4864]{2,1,0:T(8,128)(2,1)} %bitcast.59), calls=%async_computation.5 | async-start | bytes 3735552 | tf_op jit(solution)/shard_map/all_to_all | solution.py:55
  126.8 12.5 %collective-permute-done.5.refs_8_ = bf16[96,768]{1,0:T(8,128)(2,1)S(1)} collective-permute-done((bf16[96,768]{1,0:T(8,128)(2,1)S(1)}, bf16[96,768]{1,0:T(8,128)(2,1)S(1)}, u32[]{:S(2)}, u32[]{:S(2)}) %collective-permute-start.5) | collective-permute-done | bytes 147488 | tf_op jit(solution)/shard_map/ppermute | solution.py:63
  144.0 6.7 %shard_map.203 = (bf16[384,4864]{1,0:T(8,128)(2,1)}, bf16[192,128]{1,0:T(8,128)(2,1)}, bf16[192,128]{1,0:T(8,128)(2,1)}) custom-call(bf16[8,128]{1,0:T(8,128)(2,1)} %fusion.30.refs_0_, f32[24,128]{1,0:T(8,128)} %constant.67.clone.refs_1_.refs_2_, f32[48,256]{1,0:T(8,128)} %constant.69.clone.refs_2_, bf16[384,384]{1,0:T(8,128)(2,1)} %fusion.16.refs_3_, ...), custom_call_target="tpu_custom_call" | custom-call | tf_op jit(solution)/shard_map/pallas_call | solution.py:148
  150.7 7.0 %all-to-all-start = ((bf16[8,48,4864]{2,1,0:T(8,128)(2,1)}), bf16[8,48,4864]{2,1,0:T(8,128)(2,1)}, u32[]{:S(2)}, u32[]{:S(2)}) async-start(bf16[8,48,4864]{2,1,0:T(8,128)(2,1)} %bitcast.58), calls=%async_computation | async-start | bytes 7471104 | tf_op jit(solution)/shard_map/all_to_all | solution.py:55
  170.0 10.7 %shard_map.208 = (bf16[192,768]{1,0:T(8,128)(2,1)}, bf16[192,4096]{1,0:T(8,128)(2,1)}) custom-call(bf16[192,4864]{1,0:T(8,128)(2,1)} %bitcast.17.x.g0.g1.g2.refs_2_, bf16[192,4864]{1,0:T(8,128)(2,1)} %bitcast.17.x.g0.g1.g2.refs_2_, bf16[192,4864]{1,0:T(8,128)(2,1)} %bitcast.17.x.g0.g1.g2.refs_2_, bf16[192,4864]{1,0:T(8,128)(2,1)} %bitcast.17.x.g0.g1.g2.refs_2_, ...), custom_call_target="tpu_custom_call" | custom-call | flops 2415919104 | bytes 15728640 | tf_op jit(solution)/shard_map/pallas_call | solution.py:204
  180.7 11.6 %all-to-all-done = bf16[8,48,4864]{2,1,0:T(8,128)(2,1)} async-done(((bf16[8,48,4864]{2,1,0:T(8,128)(2,1)}), bf16[8,48,4864]{2,1,0:T(8,128)(2,1)}, u32[]{:S(2)}, u32[]{:S(2)}) %all-to-all-start) | async-done | bytes 3735584 | tf_op jit(solution)/shard_map/all_to_all | solution.py:55
  197.6 12.7 %shard_map.204 = (bf16[384,768]{1,0:T(8,128)(2,1)}, bf16[192,4096]{1,0:T(8,128)(2,1)}, bf16[192,4096]{1,0:T(8,128)(2,1)}) custom-call(bf16[384,4864]{1,0:T(8,128)(2,1)} %bitcast.3.x.g0.g1.g2.refs_1_, bf16[384,4864]{1,0:T(8,128)(2,1)} %bitcast.3.x.g0.g1.g2.refs_1_, bf16[384,4864]{1,0:T(8,128)(2,1)} %bitcast.3.x.g0.g1.g2.refs_1_, ...), custom_call_target="tpu_custom_call" | custom-call | flops 4831838208 | bytes 18874368 | tf_op jit(solution)/shard_map/pallas_call | solution.py:204
  210.3 7.2 %all-to-all-done.6 = bf16[8,24,4096]{2,1,0:T(8,128)(2,1)S(1)} async-done(((bf16[8,24,4096]{2,1,0:T(8,128)(2,1)}), bf16[8,24,4096]{2,1,0:T(8,128)(2,1)S(1)}, u32[]{:S(2)}, u32[]{:S(2)}) %all-to-all-start.6) | async-done | bytes 1572896 | tf_op jit(solution)/shard_map/all_to_all | solution.py:55
  218.6 5.4 %all-to-all-start.1 = ((bf16[8,24,4096]{2,1,0:T(8,128)(2,1)}), bf16[8,24,4096]{2,1,0:T(8,128)(2,1)S(1)}, u32[]{:S(2)}, u32[]{:S(2)}) async-start(bf16[8,24,4096]{2,1,0:T(8,128)(2,1)} %bitcast.63), calls=%async_computation.1 | async-start | bytes 3145728 | tf_op jit(solution)/shard_map/all_to_all | solution.py:55
  224.0 10.8 %shard_map.206 = (bf16[192,768]{1,0:T(8,128)(2,1)}, bf16[192,4096]{1,0:T(8,128)(2,1)}) custom-call(bf16[192,4864]{1,0:T(8,128)(2,1)} %bitcast.45, bf16[192,4864]{1,0:T(8,128)(2,1)} %bitcast.46, bf16[192,4864]{1,0:T(8,128)(2,1)} %bitcast.47, bf16[192,4864]{1,0:T(8,128)(2,1)} %bitcast.48, bf16[4096,768]{1,0:T(8,128)(2,1)} %fusion.7.w), custom_call_target="tpu_custom_call" | custom-call | flops 2415919104 | bytes 15728640 | tf_op jit(solution)/shard_map/pallas_call | solution.py:204
  244.1 5.4 %all-to-all-start.4 = ((bf16[8,24,4096]{2,1,0:T(8,128)(2,1)}), bf16[8,24,4096]{2,1,0:T(8,128)(2,1)}, u32[]{:S(2)}, u32[]{:S(2)}) async-start(bf16[8,24,4096]{2,1,0:T(8,128)(2,1)} %bitcast.62), calls=%async_computation.4 | async-start | bytes 3145728 | tf_op jit(solution)/shard_map/all_to_all | solution.py:55
  261.7 8.1 %collective-permute-start.19 = (bf16[64,4096]{1,0:T(8,128)(2,1)S(1)}, bf16[64,4096]{1,0:T(8,128)(2,1)S(1)}, u32[]{:S(2)}, u32[]{:S(2)}) collective-permute-start(bf16[64,4096]{1,0:T(8,128)(2,1)S(1)} %convolution_convert_fusion), channel_id=1, source_target_pairs={{0,7},{1,0},{2,1},{3,2},{4,3},{5,4},{6,5},{7,6},{8,15},{9,8},{10,9... | collective-permute-start | bytes 1572872 | tf_op jit(solution)/shard_map/ppermute | solution.py:63
  274.1 6.9 %all-to-all-start.3 = ((bf16[8,24,4096]{2,1,0:T(8,128)(2,1)}), bf16[8,24,4096]{2,1,0:T(8,128)(2,1)}, u32[]{:S(2)}, u32[]{:S(2)}) async-start(bf16[8,24,4096]{2,1,0:T(8,128)(2,1)} %bitcast.61), calls=%async_computation.3 | async-start | bytes 3145728 | tf_op jit(solution)/shard_map/all_to_all | solution.py:55
  291.9 6.4 %collective-permute-done.20 = bf16[64,4096]{1,0:T(8,128)(2,1)S(1)} collective-permute-done((bf16[64,4096]{1,0:T(8,128)(2,1)S(1)}, bf16[64,4096]{1,0:T(8,128)(2,1)S(1)}, u32[]{:S(2)}, u32[]{:S(2)}) %collective-permute-start.20) | collective-permute-done | bytes 524320 | tf_op jit(solution)/shard_map/ppermute | solution.py:63
  307.6 6.6 %adam.2 = bf16[512,768]{1,0:T(8,128)(2,1)} custom-call(bf16[1024,768]{1,0:T(8,128)(2,1)} %shard_map.209.a, bf16[1024,768]{1,0:T(8,128)(2,1)} %collective-permute-done.23.b, bf16[512,768]{1,0:T(8,128)(2,1)} %collective-permute-done.25.c, f32[1,1024,768]{2,1,0:T(8,128)} %first.3, f32[1,1024,768]{2,1,0:T(8,128)} %second.3), custom_call_target="tpu_custom_call" | custom-call | flops 4718592 | bytes 6291456 | tf_op jit(solution)/shard_map/adam/pallas_call | solution.py:33
  316.7 7.0 %collective-permute-done.27.c = bf16[512,768]{1,0:T(8,128)(2,1)} collective-permute-done((bf16[512,768]{1,0:T(8,128)(2,1)S(1)}, bf16[512,768]{1,0:T(8,128)(2,1)}, u32[]{:S(2)}, u32[]{:S(2)}) %collective-permute-start.27) | collective-permute-done | bytes 786464 | tf_op jit(solution)/shard_map/ppermute | solution.py:59
  323.7 6.6 %adam.3 = bf16[512,768]{1,0:T(8,128)(2,1)} custom-call(bf16[1024,768]{1,0:T(8,128)(2,1)} %shard_map.209.a, bf16[1024,768]{1,0:T(8,128)(2,1)} %collective-permute-done.23.b, bf16[512,768]{1,0:T(8,128)(2,1)} %collective-permute-done.27.c, f32[1,1024,768]{2,1,0:T(8,128)} %first.3, f32[1,1024,768]{2,1,0:T(8,128)} %second.3), custom_call_target="tpu_custom_call" | custom-call | flops 4718592 | bytes 6291456 | tf_op jit(solution)/shard_map/adam/pallas_call | solution.py:33
  342.7 15.3 %collective-permute-done.28 = bf16[512,768]{1,0:T(8,128)(2,1)} collective-permute-done((bf16[512,768]{1,0:T(8,128)(2,1)}, bf16[512,768]{1,0:T(8,128)(2,1)}, u32[]{:S(2)}, u32[]{:S(2)}) %collective-permute-start.28) | collective-permute-done | bytes 786464 | tf_op jit(solution)/shard_map/ppermute | solution.py:59
  (169 shorter events, 151.3 us)
Async XLA Ops:
  29.9 67.3 %all-to-all-start.2 = ((bf16[8,24,4864]{2,1,0:T(8,128)(2,1)}), bf16[8,24,4864]{2,1,0:T(8,128)(2,1)S(1)}, u32[]{:S(2)}, u32[]{:S(2)}) async-start(bf16[8,24,4864]{2,1,0:T(8,128)(2,1)} %bitcast.60), calls=%async_computation.2 | async-start | bytes 3735552 | tf_op jit(solution)/shard_map/all_to_all | solution.py:55
  53.8 55.9 %collective-permute-start.8 = (bf16[1024,768]{1,0:T(8,128)(2,1)}, bf16[1024,768]{1,0:T(8,128)(2,1)}, u32[]{:S(2)}, u32[]{:S(2)}) collective-permute-start(bf16[1024,768]{1,0:T(8,128)(2,1)} %bitcast.57), channel_id=1, source_target_pairs={{0,128},{128,0},{1,129},{129,1},{2,130},{130,2},{3,131},{131,3},{4... | collective-permute-start | bytes 4718600 | tf_op jit(solution)/shard_map/ppermute | solution.py:59
  63.1 28.6 %collective-permute-start.16 = (bf16[64,4224]{1,0:T(8,128)(2,1)S(1)}, bf16[64,4224]{1,0:T(8,128)(2,1)S(1)}, u32[]{:S(2)}, u32[]{:S(2)}) collective-permute-start(bf16[64,4224]{1,0:T(8,128)(2,1)S(1)} %collective-permute-done.15.refs_5_), channel_id=1, source_target_pairs={{0,1},{1,2},{2,3},{3,4},{4,5},{5,6},{6,7},{7,0},{8,9},{9,10},{10,1... | collective-permute-start | bytes 1622024 | tf_op jit(solution)/shard_map/ppermute | solution.py:63
  70.5 20.6 %collective-permute-start.18 = (bf16[96,768]{1,0:T(8,128)(2,1)}, bf16[96,768]{1,0:T(8,128)(2,1)S(1)}, u32[]{:S(2)}, u32[]{:S(2)}) collective-permute-start(bf16[96,768]{1,0:T(8,128)(2,1)} %get-tuple-element.32), channel_id=1, source_target_pairs={{0,3},{1,4},{2,5},{3,6},{4,7},{5,0},{6,1},{7,2},{8,11},{9,12},{10,... | collective-permute-start | bytes 442376 | tf_op jit(solution)/shard_map/ppermute | solution.py:63
  98.5 52.2 %all-to-all-start.5 = ((bf16[8,24,4864]{2,1,0:T(8,128)(2,1)}), bf16[8,24,4864]{2,1,0:T(8,128)(2,1)}, u32[]{:S(2)}, u32[]{:S(2)}) async-start(bf16[8,24,4864]{2,1,0:T(8,128)(2,1)} %bitcast.59), calls=%async_computation.5 | async-start | bytes 3735552 | tf_op jit(solution)/shard_map/all_to_all | solution.py:55
  113.6 51.0 %collective-permute-start.9 = (bf16[2,1024,768]{2,1,0:T(8,128)(2,1)}, bf16[2,1024,768]{2,1,0:T(8,128)(2,1)}, u32[]{:S(2)}, u32[]{:S(2)}) collective-permute-start(bf16[2,1024,768]{2,1,0:T(8,128)(2,1)} %pad_maximum_fusion), channel_id=1, source_target_pairs={{0,64},{64,0},{1,65},{65,1},{2,66},{66,2},{3,67},{67,3},{4,68},{68... | collective-permute-start | bytes 9437192 | tf_op jit(solution)/shard_map/ppermute | solution.py:59
  118.8 24.3 %collective-permute-start.2 = (bf16[64,4224]{1,0:T(8,128)(2,1)S(1)}, bf16[64,4224]{1,0:T(8,128)(2,1)S(1)}, u32[]{:S(2)}, u32[]{:S(2)}) collective-permute-start(bf16[64,4224]{1,0:T(8,128)(2,1)S(1)} %collective-permute-done.1.refs_6_), channel_id=1, source_target_pairs={{0,7},{1,0},{2,1},{3,2},{4,3},{5,4},{6,5},{7,6},{8,15},{9,8},{10,9... | collective-permute-start | bytes 1622024 | tf_op jit(solution)/shard_map/ppermute | solution.py:63
  121.9 21.2 %collective-permute-start.6 = (bf16[96,768]{1,0:T(8,128)(2,1)S(1)}, bf16[96,768]{1,0:T(8,128)(2,1)S(1)}, u32[]{:S(2)}, u32[]{:S(2)}) collective-permute-start(bf16[96,768]{1,0:T(8,128)(2,1)S(1)} %get-tuple-element.37), channel_id=1, source_target_pairs={{0,6},{1,7},{2,0},{3,1},{4,2},{5,3},{6,4},{7,5},{8,14},{9,15},{10,... | collective-permute-start | bytes 442376 | tf_op jit(solution)/shard_map/ppermute | solution.py:63
  150.7 41.6 %all-to-all-start = ((bf16[8,48,4864]{2,1,0:T(8,128)(2,1)}), bf16[8,48,4864]{2,1,0:T(8,128)(2,1)}, u32[]{:S(2)}, u32[]{:S(2)}) async-start(bf16[8,48,4864]{2,1,0:T(8,128)(2,1)} %bitcast.58), calls=%async_computation | async-start | bytes 7471104 | tf_op jit(solution)/shard_map/all_to_all | solution.py:55
  192.3 25.2 %all-to-all-start.6 = ((bf16[8,24,4096]{2,1,0:T(8,128)(2,1)}), bf16[8,24,4096]{2,1,0:T(8,128)(2,1)S(1)}, u32[]{:S(2)}, u32[]{:S(2)}) async-start(bf16[8,24,4096]{2,1,0:T(8,128)(2,1)} %bitcast.64), calls=%async_computation.6 | async-start | bytes 3145728 | tf_op jit(solution)/shard_map/all_to_all | solution.py:55
  218.6 25.4 %all-to-all-start.1 = ((bf16[8,24,4096]{2,1,0:T(8,128)(2,1)}), bf16[8,24,4096]{2,1,0:T(8,128)(2,1)S(1)}, u32[]{:S(2)}, u32[]{:S(2)}) async-start(bf16[8,24,4096]{2,1,0:T(8,128)(2,1)} %bitcast.63), calls=%async_computation.1 | async-start | bytes 3145728 | tf_op jit(solution)/shard_map/all_to_all | solution.py:55
  242.1 29.0 %collective-permute-start.24 = (bf16[1024,768]{1,0:T(8,128)(2,1)}, bf16[1024,768]{1,0:T(8,128)(2,1)}, u32[]{:S(2)}, u32[]{:S(2)}) collective-permute-start(bf16[1024,768]{1,0:T(8,128)(2,1)} %shard_map.212), channel_id=1, source_target_pairs={{0,64},{64,0},{1,65},{65,1},{2,66},{66,2},{3,67},{67,3},{4,68},{68... | collective-permute-start | bytes 4718600 | tf_op jit(solution)/shard_map/ppermute | solution.py:59
  244.1 30.0 %all-to-all-start.4 = ((bf16[8,24,4096]{2,1,0:T(8,128)(2,1)}), bf16[8,24,4096]{2,1,0:T(8,128)(2,1)}, u32[]{:S(2)}, u32[]{:S(2)}) async-start(bf16[8,24,4096]{2,1,0:T(8,128)(2,1)} %bitcast.62), calls=%async_computation.4 | async-start | bytes 3145728 | tf_op jit(solution)/shard_map/all_to_all | solution.py:55
  254.6 53.0 %collective-permute-start.23 = (bf16[1024,768]{1,0:T(8,128)(2,1)}, bf16[1024,768]{1,0:T(8,128)(2,1)}, u32[]{:S(2)}, u32[]{:S(2)}) collective-permute-start(bf16[1024,768]{1,0:T(8,128)(2,1)} %shard_map.210), channel_id=1, source_target_pairs={{0,64},{64,0},{1,65},{65,1},{2,66},{66,2},{3,67},{67,3},{4,68},{68... | collective-permute-start | bytes 4718600 | tf_op jit(solution)/shard_map/ppermute | solution.py:59
  261.7 19.9 %collective-permute-start.19 = (bf16[64,4096]{1,0:T(8,128)(2,1)S(1)}, bf16[64,4096]{1,0:T(8,128)(2,1)S(1)}, u32[]{:S(2)}, u32[]{:S(2)}) collective-permute-start(bf16[64,4096]{1,0:T(8,128)(2,1)S(1)} %convolution_convert_fusion), channel_id=1, source_target_pairs={{0,7},{1,0},{2,1},{3,2},{4,3},{5,4},{6,5},{7,6},{8,15},{9,8},{10,9... | collective-permute-start | bytes 1572872 | tf_op jit(solution)/shard_map/ppermute | solution.py:63
  274.1 58.3 %all-to-all-start.3 = ((bf16[8,24,4096]{2,1,0:T(8,128)(2,1)}), bf16[8,24,4096]{2,1,0:T(8,128)(2,1)}, u32[]{:S(2)}, u32[]{:S(2)}) async-start(bf16[8,24,4096]{2,1,0:T(8,128)(2,1)} %bitcast.61), calls=%async_computation.3 | async-start | bytes 3145728 | tf_op jit(solution)/shard_map/all_to_all | solution.py:55
  286.3 21.4 %collective-permute-start.25 = (bf16[512,768]{1,0:T(8,128)(2,1)S(1)}, bf16[512,768]{1,0:T(8,128)(2,1)}, u32[]{:S(2)}, u32[]{:S(2)}) collective-permute-start(bf16[512,768]{1,0:T(8,128)(2,1)S(1)} %get-tuple-element.30), channel_id=1, source_target_pairs={{0,128},{128,0},{1,129},{129,1},{2,130},{130,2},{3,131},{131,3},{4... | collective-permute-start | bytes 2359304 | tf_op jit(solution)/shard_map/ppermute | solution.py:59
  286.4 37.4 %collective-permute-start.27 = (bf16[512,768]{1,0:T(8,128)(2,1)S(1)}, bf16[512,768]{1,0:T(8,128)(2,1)}, u32[]{:S(2)}, u32[]{:S(2)}) collective-permute-start(bf16[512,768]{1,0:T(8,128)(2,1)S(1)} %get-tuple-element.31), channel_id=1, source_target_pairs={{0,128},{128,0},{1,129},{129,1},{2,130},{130,2},{3,131},{131,3},{4... | collective-permute-start | bytes 2359304 | tf_op jit(solution)/shard_map/ppermute | solution.py:59
  291.2 41.3 %collective-permute-start.13 = (bf16[64,4096]{1,0:T(8,128)(2,1)}, bf16[64,4096]{1,0:T(8,128)(2,1)}, u32[]{:S(2)}, u32[]{:S(2)}) collective-permute-start(bf16[64,4096]{1,0:T(8,128)(2,1)} %fusion.3), channel_id=1, source_target_pairs={{0,1},{1,2},{2,3},{3,4},{4,5},{5,6},{6,7},{7,0},{8,9},{9,10},{10,1... | collective-permute-start | bytes 1572872 | tf_op jit(solution)/shard_map/ppermute | solution.py:63
  301.1 34.3 %collective-permute-start.21 = (bf16[64,4096]{1,0:T(8,128)(2,1)}, bf16[64,4096]{1,0:T(8,128)(2,1)}, u32[]{:S(2)}, u32[]{:S(2)}) collective-permute-start(bf16[64,4096]{1,0:T(8,128)(2,1)} %fusion.5), channel_id=1, source_target_pairs={{0,7},{1,0},{2,1},{3,2},{4,3},{5,4},{6,5},{7,6},{8,15},{9,8},{10,9... | collective-permute-start | bytes 1572872 | tf_op jit(solution)/shard_map/ppermute | solution.py:63
  314.2 28.4 %collective-permute-start.26 = (bf16[512,768]{1,0:T(8,128)(2,1)}, bf16[512,768]{1,0:T(8,128)(2,1)S(1)}, u32[]{:S(2)}, u32[]{:S(2)}) collective-permute-start(bf16[512,768]{1,0:T(8,128)(2,1)} %adam.2), channel_id=1, source_target_pairs={{0,32},{32,0},{1,33},{33,1},{2,34},{34,2},{3,35},{35,3},{4,36},{36... | collective-permute-start | bytes 2359304 | tf_op jit(solution)/shard_map/ppermute | solution.py:59
  330.3 27.7 %collective-permute-start.28 = (bf16[512,768]{1,0:T(8,128)(2,1)}, bf16[512,768]{1,0:T(8,128)(2,1)}, u32[]{:S(2)}, u32[]{:S(2)}) collective-permute-start(bf16[512,768]{1,0:T(8,128)(2,1)} %adam.3), channel_id=1, source_target_pairs={{0,32},{32,0},{1,33},{33,1},{2,34},{34,2},{3,35},{35,3},{4,36},{36... | collective-permute-start | bytes 2359304 | tf_op jit(solution)/shard_map/ppermute | solution.py:59
  334.5 26.0 %collective-permute-start.14 = (bf16[64,4096]{1,0:T(8,128)(2,1)S(1)}, bf16[64,4096]{1,0:T(8,128)(2,1)S(1)}, u32[]{:S(2)}, u32[]{:S(2)}) collective-permute-start(bf16[64,4096]{1,0:T(8,128)(2,1)S(1)} %fusion.2), channel_id=1, source_target_pairs={{0,1},{1,2},{2,3},{3,4},{4,5},{5,6},{6,7},{7,0},{8,9},{9,10},{10,1... | collective-permute-start | bytes 1572872 | tf_op jit(solution)/shard_map/ppermute | solution.py:63
  337.3 23.2 %collective-permute-start.22 = (bf16[64,4096]{1,0:T(8,128)(2,1)S(1)}, bf16[64,4096]{1,0:T(8,128)(2,1)S(1)}, u32[]{:S(2)}, u32[]{:S(2)}) collective-permute-start(bf16[64,4096]{1,0:T(8,128)(2,1)S(1)} %fusion.4), channel_id=1, source_target_pairs={{0,7},{1,0},{2,1},{3,2},{4,3},{5,4},{6,5},{7,6},{8,15},{9,8},{10,9... | collective-permute-start | bytes 1572872 | tf_op jit(solution)/shard_map/ppermute | solution.py:63
  (48 other events, 440.4 us)
where the time goes:
time: 365 us; the launch traced here: 362 us
  waiting for transfers between devices  125 us (34%)
  starting transfers between devices  95.7 us (26%)
  Pallas kernels  84.2 us (23%)
  local copies, waits for them, and re-layouts  22.8 us (6%)
  matrix products  17.5 us (5%)
  other arithmetic  15.6 us (4%)
    ppermute x21, waiting for transfers between devices, shifted(): lax.ppermute(block, 'z', [(i, (i + by) % PLANES) for i in range(PLANES)])  77.5 us
    ppermute x21, starting transfers between devices, shifted(): lax.ppermute(block, 'z', [(i, (i + by) % PLANES) for i in range(PLANES)])  46.1 us
    all_to_all x7, starting transfers between devices, exchange_plane(): lax.all_to_all(block, ('xl', 'xh', 'y'), 0, 0, axis_index_groups=groups,...  43.8 us
    pallas_call x3, Pallas kernels, expert(): pl.pallas_call(functools.partial(expert_kernel, nk), grid=(2, nk), in_spe...  34.1 us
    ppermute x8, waiting for transfers between devices, swapped(): return lax.ppermute(block, axis, [(0, 1), (1, 0)])  26.3 us
    pallas_call x4, Pallas kernels, weight_grad(): pl.pallas_call(functools.partial(dw_kernel, len(xs)), grid_spec=pltpu.Pre...  20.8 us
    all_to_all x7, waiting for transfers between devices, exchange_plane(): lax.all_to_all(block, ('xl', 'xh', 'y'), 0, 0, axis_index_groups=groups,...  20.7 us
    dot_general x10, matrix products, dot(): lax.dot_general(a, b, (contract, ((), ())), preferred_element_type=jnp.fl...  17.5 us
  transfers between devices with their start and end apart: 36, of which 17 were waited for; matrix products, arithmetic and copies ran while one was open for 12% of the time, Pallas kernels for 22%

commit v1 on v0

--- a/solution.py
+++ b/solution.py
@@ -11,29 +11,36 @@
 CAP = 12
 PLANES = 8
 LANES = 8
-GROUPS = ((-1, 1), (3, 0, 2, -2), (-4, -3))
-BACK = ((1, 0), (2, 0), (1, 1), (0, 0))
+GROUPS = ((-1, 1), (-2, 2), (-4, 3, -3, 0))
+BACK = ((1, 0), (2, 0), (2, 1), (0, 0))
 SWAP_PARTS = 2
 
 
 def adam_kernel(a, b, c, first, second, out):
-    grad = a[...].astype(jnp.float32) + b[...].astype(jnp.float32) + c[...].astype(jnp.float32)
-    first_new = 0.9 * first[0] + 0.1 * grad
-    second_new = 0.95 * second[0] + 0.05 * grad * grad
-    out[...] = (first_new / (jnp.sqrt(second_new) + 1e-08)).astype(out.dtype)
+    bn = 64
+
+    def rows(i, carry):
+        at = pl.ds(pl.multiple_of(i * bn, bn), bn)
+        grad = a[0, at].astype(jnp.float32) + b[0, at].astype(jnp.float32)
+        grad = grad + c[at].astype(jnp.float32)
+        first_new = 0.9 * first[0, at] + 0.1 * grad
+        second_new = 0.95 * second[0, at] + 0.05 * grad * grad
+        out[at] = (first_new / (jnp.sqrt(second_new) + 1e-08)).astype(out.dtype)
+        return carry
+
+    lax.fori_loop(0, out.shape[0] // bn, rows, 0)
 
 
 def adam_direction(own, from_core, from_x, first, second, part):
     rows, hidden = from_x.shape
-    bn = 64
+    bn = 256
     skip = part * (rows // bn)
-    here = pl.BlockSpec((bn, hidden), lambda i: (i + skip, 0))
+    long = pl.BlockSpec((1, bn, hidden), lambda i: (0, i + skip, 0))
     short = pl.BlockSpec((bn, hidden), lambda i: (i, 0))
-    moment = pl.BlockSpec((1, bn, hidden), lambda i: (0, i + skip, 0))
     return pl.pallas_call(
         adam_kernel,
         grid=(rows // bn,),
-        in_specs=[here, here, short, moment, moment],
+        in_specs=[long, long, short, long, long],
         out_specs=short,
         out_shape=jax.ShapeDtypeStruct((rows, hidden), jnp.bfloat16),
         cost_estimate=pl.CostEstimate(
@@ -69,32 +76,34 @@
     for x in xs:
         joined[pl.ds(at, x.shape[0]), :] = x[...]
         at += x.shape[0]
-    out[...] = dot(joined[...], g[...], ((0,), (0,))).astype(out.dtype)
-
-
-def weight_grad(me, xs, g, other):
+    out[0] = dot(joined[...], g[...], ((0,), (0,))).astype(out.dtype)
+
+
+def weight_grad(me, xs, g, odd):
     rows, hidden = g.shape
     width = xs[0].shape[1] - hidden
     shard = width // 4
-    bn = 256
+    bn = 512
     per = shard // bn
     spec = [
-        pl.BlockSpec((x.shape[0], bn), lambda i, m: (0, jnp.bitwise_xor(m[0], other) * per + i))
+        pl.BlockSpec(
+            (x.shape[0], bn), lambda h, i, m: (0, jnp.bitwise_xor(2 * h + odd, m[0]) * per + i)
+        )
         for x in xs
     ]
     return pl.pallas_call(
         functools.partial(dw_kernel, len(xs)),
         grid_spec=pltpu.PrefetchScalarGridSpec(
             num_scalar_prefetch=1,
-            grid=(per,),
-            in_specs=spec + [pl.BlockSpec(g.shape, lambda i, m: (0, 0))],
-            out_specs=pl.BlockSpec((bn, hidden), lambda i, m: (i, 0)),
+            grid=(2, per),
+            in_specs=spec + [pl.BlockSpec(g.shape, lambda h, i, m: (0, 0))],
+            out_specs=pl.BlockSpec((1, bn, hidden), lambda h, i, m: (h, i, 0)),
             scratch_shapes=[pltpu.VMEM((rows, bn), jnp.bfloat16)],
         ),
-        out_shape=jax.ShapeDtypeStruct((shard, hidden), jnp.bfloat16),
+        out_shape=jax.ShapeDtypeStruct((2, shard, hidden), jnp.bfloat16),
         cost_estimate=pl.CostEstimate(
-            flops=2 * rows * shard * hidden,
-            bytes_accessed=2 * (rows * shard + shard * hidden + g.size),
+            flops=4 * rows * shard * hidden,
+            bytes_accessed=2 * (2 * rows * shard + 2 * shard * hidden + g.size),
             transcendentals=0,
         ),
     )(me, *xs, g)
@@ -281,36 +290,35 @@
         grads.append(grad)
         backs.append(back)
 
-    going = {}
+    part = {}
     for n, h in BACK:
         back = exchange_plane(backs[n][h].reshape(LANES, pair, width))
         back = back.reshape(LANES * pair, width)
         for i, s in enumerate(GROUPS[n][2 * h : 2 * h + 2]):
-            sign = 1 if s > 0 else -1
-            part = dot(picks[n][h][:, i * tok_dev : (i + 1) * tok_dev], back, ((0,), (0,)))
-            if s == 0:
-                home = part
-                continue
-            if sign in going:
-                part = part + going[sign].astype(f32)
-            going[sign] = shifted(part.astype(bf16), sign)
-    token_grad = (home + going[1].astype(f32) + going[-1].astype(f32)).astype(bf16)
+            mine = picks[n][h][:, i * tok_dev : (i + 1) * tok_dev]
+            part[s] = dot(mine, back, ((0,), (0,)))
+    arrived = []
+    for far, sign in ((-4, 1), (3, -1)):
+        going = None
+        for s in range(far, 0, sign):
+            total = part[s] if going is None else part[s] + going.astype(f32)
+            going = shifted(total.astype(bf16), -sign)
+        arrived.append(going.astype(f32))
+    token_grad = (part[0] + arrived[0] + arrived[1]).astype(bf16)
 
     grad_rows = jnp.concatenate(grads, axis=0)
     me_ref = me.astype(i32).reshape(1)
-    block = {}
-    for other in (3, 2, 1, 0):
-        block[other] = weight_grad(me_ref, xs, grad_rows, other)
-    from_core_x = swapped(block[3], "core")
-    from_core = swapped(block[1], "core")
-    other = (block[2].astype(f32) + from_core_x.astype(f32)).astype(bf16)
+    to_core = weight_grad(me_ref, xs, grad_rows, 1)
+    from_core = swapped(to_core, "core")
+    kept = weight_grad(me_ref, xs, grad_rows, 0)
+    other = (kept[1].astype(f32) + from_core[1].astype(f32)).astype(bf16)
     moving = jnp.sum(jnp.where(jnp.arange(slots, dtype=i32) == here, swap_mask, 0)) == 1
     size = shard // SWAP_PARTS
     steps = []
     for s in range(SWAP_PARTS):
         at = slice(s * size, (s + 1) * size)
         from_x = swapped(other[at], "xl")
-        stepped = adam_direction(block[0], from_core, from_x, first_moment, second_moment, s)
+        stepped = adam_direction(kept, from_core, from_x, first_moment, second_moment, s)
         partner = swapped(stepped, "xh")
         steps.append(jnp.where(moving, partner, stepped))
     adam_step = jnp.concatenate(steps, axis=0)[None]

time: 365 us -> 362 us (level)
  Pallas kernels: 84.2 us -> 71.3 us
  waiting for transfers between devices: 125 us -> 134 us
  starting transfers between devices: 95.7 us -> 89.7 us
  local copies, waits for them, and re-layouts: 22.8 us -> 28.7 us
    ppermute x21, waiting for transfers between devices: 77.5 us -> 64.3 us  [shifted(): lax.ppermute(block, 'z', [(i, (i + by) % PLANES) for i in range(PLANES)])]
    ppermute x8 -> x7, waiting for transfers between devices: 26.3 us -> 39.3 us  [swapped(): return lax.ppermute(block, axis, [(0, 1), (1, 0)])]
    all_to_all x7, waiting for transfers between devices: 20.7 us -> 30.5 us  [exchange_plane(): lax.all_to_all(block, ('xl', 'xh', 'y'), 0, 0, axis_index_groups=groups,...]
    pallas_call x4 -> x2, Pallas kernels: 20.8 us -> 13.2 us  [weight_grad(): pl.pallas_call(functools.partial(dw_kernel, len(xs)), grid_spec=pltpu.Pre...]
    ppermute x21, starting transfers between devices: 46.1 us -> 39.1 us  [shifted(): lax.ppermute(block, 'z', [(i, (i + by) % PLANES) for i in range(PLANES)])]
    pallas_call x2, Pallas kernels: 13.2 us -> 7.9 us  [adam_direction(): pl.pallas_call(adam_kernel, grid=(rows // bn,), in_specs=[long, long, sho...]
    unnamed x75 -> x77, local copies, waits for them, and re-layouts: 9.45 us -> 12.4 us
  transfers between devices with their start and end apart: 36 -> 35, of which waited for: 17 -> 17; matrix products, arithmetic and copies ran while one was open for 12% -> 13% of each run, Pallas kernels for 22% -> 19%
where the time goes in v1:
time: 362 us; the launch traced here: 357 us
  waiting for transfers between devices  134 us (37%)
  starting transfers between devices  89.7 us (25%)
  Pallas kernels  71.3 us (20%)
  local copies, waits for them, and re-layouts  28.7 us (8%)
  matrix products  18.7 us (5%)
  other arithmetic  12.9 us (4%)
    ppermute x21, waiting for transfers between devices, shifted(): lax.ppermute(block, 'z', [(i, (i + by) % PLANES) for i in range(PLANES)])  64.3 us
    all_to_all x7, starting transfers between devices, exchange_plane(): lax.all_to_all(block, ('xl', 'xh', 'y'), 0, 0, axis_index_groups=groups,...  44.1 us
    ppermute x7, waiting for transfers between devices, swapped(): return lax.ppermute(block, axis, [(0, 1), (1, 0)])  39.3 us
    ppermute x21, starting transfers between devices, shifted(): lax.ppermute(block, 'z', [(i, (i + by) % PLANES) for i in range(PLANES)])  39.1 us
    pallas_call x3, Pallas kernels, expert(): pl.pallas_call(functools.partial(expert_kernel, nk), grid=(2, nk), in_spe...  34.1 us
    all_to_all x7, waiting for transfers between devices, exchange_plane(): lax.all_to_all(block, ('xl', 'xh', 'y'), 0, 0, axis_index_groups=groups,...  30.5 us
    dot_general x10, matrix products, dot(): lax.dot_general(a, b, (contract, ((), ())), preferred_element_type=jnp.fl...  18.7 us
    pallas_call x3, Pallas kernels, pack(): pl.pallas_call(functools.partial(pack_kernel, count), out_shape=[jax.Shap...  16 us
  transfers between devices with their start and end apart: 35, of which 17 were waited for; matrix products, arithmetic and copies ran while one was open for 13% of the time, Pallas kernels for 19%

profile of v1, /device:TPU:120, one launch (start us, length us, event | category | flops | bytes accessed | tf_op | source)
XLA Modules:
  0.0 356.8 jit_solution(4683661431486765573)
XLA Ops:
  15.5 7.3 %collective-permute-done.12.refs_6_ = bf16[96,768]{1,0:T(8,128)(2,1)S(1)} collective-permute-done((bf16[96,768]{1,0:T(8,128)(2,1)S(1)}, bf16[96,768]{1,0:T(8,128)(2,1)S(1)}, u32[]{:S(2)}, u32[]{:S(2)}) %collective-permute-start.12) | collective-permute-done | bytes 147488 | tf_op jit(solution)/shard_map/ppermute | solution.py:70
  32.7 7.0 %all-to-all-start.2 = ((bf16[8,24,4864]{2,1,0:T(8,128)(2,1)}), bf16[8,24,4864]{2,1,0:T(8,128)(2,1)S(1)}, u32[]{:S(2)}, u32[]{:S(2)}) async-start(bf16[8,24,4864]{2,1,0:T(8,128)(2,1)} %bitcast.68), calls=%async_computation.2 | async-start | bytes 3735552 | tf_op jit(solution)/shard_map/all_to_all | solution.py:62
  41.7 10.6 %collective-permute-done.1.refs_4_ = bf16[64,4224]{1,0:T(8,128)(2,1)S(1)} collective-permute-done((bf16[64,4224]{1,0:T(8,128)(2,1)}, bf16[64,4224]{1,0:T(8,128)(2,1)S(1)}, u32[]{:S(2)}, u32[]{:S(2)}) %collective-permute-start.1) | collective-permute-done | bytes 540704 | tf_op jit(solution)/shard_map/ppermute | solution.py:70
  54.6 10.1 %collective-permute-done.2.refs_6_ = bf16[64,4224]{1,0:T(8,128)(2,1)S(1)} collective-permute-done((bf16[64,4224]{1,0:T(8,128)(2,1)S(1)}, bf16[64,4224]{1,0:T(8,128)(2,1)S(1)}, u32[]{:S(2)}, u32[]{:S(2)}) %collective-permute-start.2) | collective-permute-done | bytes 540704 | tf_op jit(solution)/shard_map/ppermute | solution.py:70
  70.4 10.3 %collective-permute-done.7.refs_8_ = bf16[96,768]{1,0:T(8,128)(2,1)} collective-permute-done((bf16[96,768]{1,0:T(8,128)(2,1)}, bf16[96,768]{1,0:T(8,128)(2,1)}, u32[]{:S(2)}, u32[]{:S(2)}) %collective-permute-start.7) | collective-permute-done | bytes 147488 | tf_op jit(solution)/shard_map/ppermute | solution.py:70
  80.7 10.5 %collective-permute-start.9 = (bf16[96,768]{1,0:T(8,128)(2,1)}, bf16[96,768]{1,0:T(8,128)(2,1)S(1)}, u32[]{:S(2)}, u32[]{:S(2)}) collective-permute-start(bf16[96,768]{1,0:T(8,128)(2,1)} %get-tuple-element.37), channel_id=1, source_target_pairs={{0,3},{1,4},{2,5},{3,6},{4,7},{5,0},{6,1},{7,2},{8,11},{9,12},{10,... | collective-permute-start | bytes 442376 | tf_op jit(solution)/shard_map/ppermute | solution.py:70
  95.9 6.6 %shard_map.203 = (bf16[384,4864]{1,0:T(8,128)(2,1)}, bf16[192,128]{1,0:T(8,128)(2,1)}, bf16[192,128]{1,0:T(8,128)(2,1)}) custom-call(bf16[8,128]{1,0:T(8,128)(2,1)} %fusion.30.refs_0_, f32[24,128]{1,0:T(8,128)} %constant.67.clone.refs_1_.refs_2_, f32[48,256]{1,0:T(8,128)} %constant.69.clone.refs_2_, bf16[384,384]{1,0:T(8,128)(2,1)} %fusion.16.refs_3_, ...), custom_call_target="tpu_custom_call" | custom-call | tf_op jit(solution)/shard_map/pallas_call | solution.py:157
  103.8 6.9 %all-to-all-start = ((bf16[8,48,4864]{2,1,0:T(8,128)(2,1)}), bf16[8,48,4864]{2,1,0:T(8,128)(2,1)}, u32[]{:S(2)}, u32[]{:S(2)}) async-start(bf16[8,48,4864]{2,1,0:T(8,128)(2,1)} %bitcast.66), calls=%async_computation | async-start | bytes 7471104 | tf_op jit(solution)/shard_map/all_to_all | solution.py:62
  117.0 5.4 %collective-permute-done.14.refs_6_ = bf16[96,768]{1,0:T(8,128)(2,1)S(1)} collective-permute-done((bf16[96,768]{1,0:T(8,128)(2,1)S(1)}, bf16[96,768]{1,0:T(8,128)(2,1)S(1)}, u32[]{:S(2)}, u32[]{:S(2)}) %collective-permute-start.14) | collective-permute-done | bytes 147488 | tf_op jit(solution)/shard_map/ppermute | solution.py:70
  128.5 18.5 %all-to-all-done = bf16[8,48,4864]{2,1,0:T(8,128)(2,1)} async-done(((bf16[8,48,4864]{2,1,0:T(8,128)(2,1)}), bf16[8,48,4864]{2,1,0:T(8,128)(2,1)}, u32[]{:S(2)}, u32[]{:S(2)}) %all-to-all-start) | async-done | bytes 3735584 | tf_op jit(solution)/shard_map/all_to_all | solution.py:62
  164.7 12.7 %shard_map.204 = (bf16[384,768]{1,0:T(8,128)(2,1)}, bf16[192,4096]{1,0:T(8,128)(2,1)}, bf16[192,4096]{1,0:T(8,128)(2,1)}) custom-call(bf16[384,4864]{1,0:T(8,128)(2,1)} %bitcast.3.x.g0.g1.g2.refs_2_, bf16[384,4864]{1,0:T(8,128)(2,1)} %bitcast.3.x.g0.g1.g2.refs_2_, bf16[384,4864]{1,0:T(8,128)(2,1)} %bitcast.3.x.g0.g1.g2.refs_2_, ...), custom_call_target="tpu_custom_call" | custom-call | flops 4831838208 | bytes 18874368 | tf_op jit(solution)/shard_map/pallas_call | solution.py:213
  178.7 6.9 %all-to-all-start.6 = ((bf16[8,24,4096]{2,1,0:T(8,128)(2,1)}), bf16[8,24,4096]{2,1,0:T(8,128)(2,1)S(1)}, u32[]{:S(2)}, u32[]{:S(2)}) async-start(bf16[8,24,4096]{2,1,0:T(8,128)(2,1)} %bitcast.71), calls=%async_computation.6 | async-start | bytes 3145728 | tf_op jit(solution)/shard_map/all_to_all | solution.py:62
  185.6 10.8 %shard_map.206 = (bf16[192,768]{1,0:T(8,128)(2,1)}, bf16[192,4096]{1,0:T(8,128)(2,1)}) custom-call(bf16[192,4864]{1,0:T(8,128)(2,1)} %bitcast.49, bf16[192,4864]{1,0:T(8,128)(2,1)} %bitcast.50, bf16[192,4864]{1,0:T(8,128)(2,1)} %bitcast.51, bf16[192,4864]{1,0:T(8,128)(2,1)} %bitcast.52, bf16[4096,768]{1,0:T(8,128)(2,1)} %fusion.7.w), custom_call_target="tpu_custom_call" | custom-call | flops 2415919104 | bytes 15728640 | tf_op jit(solution)/shard_map/pallas_call | solution.py:213
  198.1 10.7 %shard_map.208 = (bf16[192,768]{1,0:T(8,128)(2,1)}, bf16[192,4096]{1,0:T(8,128)(2,1)}) custom-call(bf16[192,4864]{1,0:T(8,128)(2,1)} %bitcast.55, bf16[192,4864]{1,0:T(8,128)(2,1)} %bitcast.56, bf16[192,4864]{1,0:T(8,128)(2,1)} %bitcast.57, bf16[192,4864]{1,0:T(8,128)(2,1)} %bitcast.58, bf16[4096,768]{1,0:T(8,128)(2,1)} %fusion.7.w), custom_call_target="tpu_custom_call" | custom-call | flops 2415919104 | bytes 15728640 | tf_op jit(solution)/shard_map/pallas_call | solution.py:213
  208.7 7.1 %all-to-all-start.1 = ((bf16[8,24,4096]{2,1,0:T(8,128)(2,1)}), bf16[8,24,4096]{2,1,0:T(8,128)(2,1)S(1)}, u32[]{:S(2)}, u32[]{:S(2)}) async-start(bf16[8,24,4096]{2,1,0:T(8,128)(2,1)} %bitcast.70), calls=%async_computation.1 | async-start | bytes 3145728 | tf_op jit(solution)/shard_map/all_to_all | solution.py:62
  218.5 6.6 %shard_map.210 = bf16[2,1024,768]{2,1,0:T(8,128)(2,1)} custom-call(s32[1]{0:T(128)} %bitcast.20.me, bf16[192,4864]{1,0:T(8,128)(2,1)} %bitcast.53, bf16[192,4864]{1,0:T(8,128)(2,1)} %bitcast.59, bf16[384,4864]{1,0:T(8,128)(2,1)} %bitcast.3.x.g0.g1.g2.refs_2_, bf16[768,768]{1,0:T(8,128)(2,1)} %constant_dynamic-update-slice_fusion.refs_3_), custom_call_target="tpu_custom_call" | custom-call | flops 2415919104 | bytes 7471104 | tf_op jit(solution)/shard_map/pallas_call | solution.py:94
  225.0 9.5 %all-to-all-done.1 = bf16[8,24,4096]{2,1,0:T(8,128)(2,1)S(1)} async-done(((bf16[8,24,4096]{2,1,0:T(8,128)(2,1)}), bf16[8,24,4096]{2,1,0:T(8,128)(2,1)S(1)}, u32[]{:S(2)}, u32[]{:S(2)}) %all-to-all-start.1) | async-done | bytes 1572896 | tf_op jit(solution)/shard_map/all_to_all | solution.py:62
  234.6 5.5 %all-to-all-start.5 = ((bf16[8,24,4096]{2,1,0:T(8,128)(2,1)}), bf16[8,24,4096]{2,1,0:T(8,128)(2,1)}, u32[]{:S(2)}, u32[]{:S(2)}) async-start(bf16[8,24,4096]{2,1,0:T(8,128)(2,1)} %bitcast.69), calls=%async_computation.5 | async-start | bytes 3145728 | tf_op jit(solution)/shard_map/all_to_all | solution.py:62
  245.1 9.9 %collective-permute-done.16 = bf16[64,4096]{1,0:T(8,128)(2,1)S(1)} collective-permute-done((bf16[64,4096]{1,0:T(8,128)(2,1)S(1)}, bf16[64,4096]{1,0:T(8,128)(2,1)S(1)}, u32[]{:S(2)}, u32[]{:S(2)}) %collective-permute-start.16) | collective-permute-done | bytes 524320 | tf_op jit(solution)/shard_map/ppermute | solution.py:70
  265.6 6.6 %shard_map.209.a = bf16[2,1024,768]{2,1,0:T(8,128)(2,1)} custom-call(s32[1]{0:T(128)} %bitcast.20.me, bf16[192,4864]{1,0:T(8,128)(2,1)} %bitcast.54, bf16[192,4864]{1,0:T(8,128)(2,1)} %bitcast.60, bf16[384,4864]{1,0:T(8,128)(2,1)} %bitcast.3.x.g0.g1.g2.refs_2_, bf16[768,768]{1,0:T(8,128)(2,1)} %constant_dynamic-update-slice_fusion.refs_3_), custom_call_target="tpu_custom_call" | custom-call | flops 2415919104 | bytes 7471104 | tf_op jit(solution)/shard_map/pallas_call | solution.py:94
  298.2 6.4 %collective-permute-done.24.c = bf16[512,768]{1,0:T(8,128)(2,1)S(1)} collective-permute-done((bf16[512,768]{1,0:T(8,128)(2,1)S(1)}, bf16[512,768]{1,0:T(8,128)(2,1)S(1)}, u32[]{:S(2)}, u32[]{:S(2)}) %collective-permute-start.24) | collective-permute-done | bytes 786464 | tf_op jit(solution)/shard_map/ppermute | solution.py:66
  311.7 9.8 %collective-permute-done.26.c = bf16[512,768]{1,0:T(8,128)(2,1)S(1)} collective-permute-done((bf16[512,768]{1,0:T(8,128)(2,1)}, bf16[512,768]{1,0:T(8,128)(2,1)S(1)}, u32[]{:S(2)}, u32[]{:S(2)}) %collective-permute-start.26) | collective-permute-done | bytes 786464 | tf_op jit(solution)/shard_map/ppermute | solution.py:66
  332.3 8.1 %collective-permute-done.25 = bf16[512,768]{1,0:T(8,128)(2,1)S(1)} collective-permute-done((bf16[512,768]{1,0:T(8,128)(2,1)}, bf16[512,768]{1,0:T(8,128)(2,1)S(1)}, u32[]{:S(2)}, u32[]{:S(2)}) %collective-permute-start.25) | collective-permute-done | bytes 786464 | tf_op jit(solution)/shard_map/ppermute | solution.py:66
  340.5 15.0 %collective-permute-done.27 = bf16[512,768]{1,0:T(8,128)(2,1)S(1)} collective-permute-done((bf16[512,768]{1,0:T(8,128)(2,1)}, bf16[512,768]{1,0:T(8,128)(2,1)S(1)}, u32[]{:S(2)}, u32[]{:S(2)}) %collective-permute-start.27) | collective-permute-done | bytes 786464 | tf_op jit(solution)/shard_map/ppermute | solution.py:66
  (167 shorter events, 136.4 us)
Async XLA Ops:
  4.9 21.3 %collective-permute-start = (bf16[64,4224]{1,0:T(8,128)(2,1)S(1)}, bf16[64,4224]{1,0:T(8,128)(2,1)S(1)}, u32[]{:S(2)}, u32[]{:S(2)}) collective-permute-start(bf16[64,4224]{1,0:T(8,128)(2,1)S(1)} %fusion.17.refs_7_), channel_id=1, source_target_pairs={{0,1},{1,2},{2,3},{3,4},{4,5},{5,6},{6,7},{7,0},{8,9},{9,10},{10,1... | collective-permute-start | bytes 1622024 | tf_op jit(solution)/shard_map/ppermute | solution.py:70
  8.1 18.1 %collective-permute-start.4 = (bf16[64,4224]{1,0:T(8,128)(2,1)S(1)}, bf16[64,4224]{1,0:T(8,128)(2,1)S(1)}, u32[]{:S(2)}, u32[]{:S(2)}) collective-permute-start(bf16[64,4224]{1,0:T(8,128)(2,1)S(1)} %fusion.17.refs_7_), channel_id=1, source_target_pairs={{0,7},{1,0},{2,1},{3,2},{4,3},{5,4},{6,5},{7,6},{8,15},{9,8},{10,9... | collective-permute-start | bytes 1622024 | tf_op jit(solution)/shard_map/ppermute | solution.py:70
  32.7 69.8 %all-to-all-start.2 = ((bf16[8,24,4864]{2,1,0:T(8,128)(2,1)}), bf16[8,24,4864]{2,1,0:T(8,128)(2,1)S(1)}, u32[]{:S(2)}, u32[]{:S(2)}) async-start(bf16[8,24,4864]{2,1,0:T(8,128)(2,1)} %bitcast.68), calls=%async_computation.2 | async-start | bytes 3735552 | tf_op jit(solution)/shard_map/all_to_all | solution.py:62
  54.1 56.6 %collective-permute-start.10 = (bf16[1024,768]{1,0:T(8,128)(2,1)S(1)}, bf16[1024,768]{1,0:T(8,128)(2,1)}, u32[]{:S(2)}, u32[]{:S(2)}) collective-permute-start(bf16[1024,768]{1,0:T(8,128)(2,1)S(1)} %bitcast.65), channel_id=1, source_target_pairs={{0,128},{128,0},{1,129},{129,1},{2,130},{130,2},{3,131},{131,3},{4... | collective-permute-start | bytes 4718600 | tf_op jit(solution)/shard_map/ppermute | solution.py:66
  54.3 39.9 %collective-permute-start.6 = (bf16[64,4224]{1,0:T(8,128)(2,1)S(1)}, bf16[64,4224]{1,0:T(8,128)(2,1)S(1)}, u32[]{:S(2)}, u32[]{:S(2)}) collective-permute-start(bf16[64,4224]{1,0:T(8,128)(2,1)S(1)} %collective-permute-done.5.refs_5_), channel_id=1, source_target_pairs={{0,7},{1,0},{2,1},{3,2},{4,3},{5,4},{6,5},{7,6},{8,15},{9,8},{10,9... | collective-permute-start | bytes 1622024 | tf_op jit(solution)/shard_map/ppermute | solution.py:70
  64.7 29.5 %collective-permute-start.3 = (bf16[64,4224]{1,0:T(8,128)(2,1)S(1)}, bf16[64,4224]{1,0:T(8,128)(2,1)S(1)}, u32[]{:S(2)}, u32[]{:S(2)}) collective-permute-start(bf16[64,4224]{1,0:T(8,128)(2,1)S(1)} %collective-permute-done.2.refs_6_), channel_id=1, source_target_pairs={{0,1},{1,2},{2,3},{3,4},{4,5},{5,6},{6,7},{7,0},{8,9},{9,10},{10,1... | collective-permute-start | bytes 1622024 | tf_op jit(solution)/shard_map/ppermute | solution.py:70
  69.2 22.8 %collective-permute-start.8 = (bf16[96,768]{1,0:T(8,128)(2,1)}, bf16[96,768]{1,0:T(8,128)(2,1)S(1)}, u32[]{:S(2)}, u32[]{:S(2)}) collective-permute-start(bf16[96,768]{1,0:T(8,128)(2,1)} %get-tuple-element.38), channel_id=1, source_target_pairs={{0,5},{1,6},{2,7},{3,0},{4,1},{5,2},{6,3},{7,4},{8,13},{9,14},{10,... | collective-permute-start | bytes 442376 | tf_op jit(solution)/shard_map/ppermute | solution.py:70
  103.8 43.3 %all-to-all-start = ((bf16[8,48,4864]{2,1,0:T(8,128)(2,1)}), bf16[8,48,4864]{2,1,0:T(8,128)(2,1)}, u32[]{:S(2)}, u32[]{:S(2)}) async-start(bf16[8,48,4864]{2,1,0:T(8,128)(2,1)} %bitcast.66), calls=%async_computation | async-start | bytes 7471104 | tf_op jit(solution)/shard_map/all_to_all | solution.py:62
  114.1 45.3 %collective-permute-start.11 = (bf16[2,1024,768]{2,1,0:T(8,128)(2,1)}, bf16[2,1024,768]{2,1,0:T(8,128)(2,1)}, u32[]{:S(2)}, u32[]{:S(2)}) collective-permute-start(bf16[2,1024,768]{2,1,0:T(8,128)(2,1)} %pad_maximum_fusion), channel_id=1, source_target_pairs={{0,64},{64,0},{1,65},{65,1},{2,66},{66,2},{3,67},{67,3},{4,68},{68... | collective-permute-start | bytes 9437192 | tf_op jit(solution)/shard_map/ppermute | solution.py:66
  147.1 30.4 %all-to-all-start.4 = ((bf16[8,24,4864]{2,1,0:T(8,128)(2,1)}), bf16[8,24,4864]{2,1,0:T(8,128)(2,1)S(1)}, u32[]{:S(2)}, u32[]{:S(2)}) async-start(bf16[8,24,4864]{2,1,0:T(8,128)(2,1)} %bitcast.67), calls=%async_computation.4 | async-start | bytes 3735552 | tf_op jit(solution)/shard_map/all_to_all | solution.py:62
  178.7 30.0 %all-to-all-start.6 = ((bf16[8,24,4096]{2,1,0:T(8,128)(2,1)}), bf16[8,24,4096]{2,1,0:T(8,128)(2,1)S(1)}, u32[]{:S(2)}, u32[]{:S(2)}) async-start(bf16[8,24,4096]{2,1,0:T(8,128)(2,1)} %bitcast.71), calls=%async_computation.6 | async-start | bytes 3145728 | tf_op jit(solution)/shard_map/all_to_all | solution.py:62
  208.7 25.8 %all-to-all-start.1 = ((bf16[8,24,4096]{2,1,0:T(8,128)(2,1)}), bf16[8,24,4096]{2,1,0:T(8,128)(2,1)S(1)}, u32[]{:S(2)}, u32[]{:S(2)}) async-start(bf16[8,24,4096]{2,1,0:T(8,128)(2,1)} %bitcast.70), calls=%async_computation.1 | async-start | bytes 3145728 | tf_op jit(solution)/shard_map/all_to_all | solution.py:62
  225.0 56.4 %collective-permute-start.23 = (bf16[2,1024,768]{2,1,0:T(8,128)(2,1)}, bf16[2,1024,768]{2,1,0:T(8,128)(2,1)}, u32[]{:S(2)}, u32[]{:S(2)}) collective-permute-start(bf16[2,1024,768]{2,1,0:T(8,128)(2,1)} %shard_map.210), channel_id=1, source_target_pairs={{0,64},{64,0},{1,65},{65,1},{2,66},{66,2},{3,67},{67,3},{4,68},{68... | collective-permute-start | bytes 9437192 | tf_op jit(solution)/shard_map/ppermute | solution.py:66
  234.6 25.7 %all-to-all-start.5 = ((bf16[8,24,4096]{2,1,0:T(8,128)(2,1)}), bf16[8,24,4096]{2,1,0:T(8,128)(2,1)}, u32[]{:S(2)}, u32[]{:S(2)}) async-start(bf16[8,24,4096]{2,1,0:T(8,128)(2,1)} %bitcast.69), calls=%async_computation.5 | async-start | bytes 3145728 | tf_op jit(solution)/shard_map/all_to_all | solution.py:62
  244.5 27.7 %collective-permute-start.20 = (bf16[64,4096]{1,0:T(8,128)(2,1)}, bf16[64,4096]{1,0:T(8,128)(2,1)S(1)}, u32[]{:S(2)}, u32[]{:S(2)}) collective-permute-start(bf16[64,4096]{1,0:T(8,128)(2,1)} %convolution_convert_fusion), channel_id=1, source_target_pairs={{0,1},{1,2},{2,3},{3,4},{4,5},{5,6},{6,7},{7,0},{8,9},{9,10},{10,1... | collective-permute-start | bytes 1572872 | tf_op jit(solution)/shard_map/ppermute | solution.py:70
  256.4 21.4 %collective-permute-start.17 = (bf16[64,4096]{1,0:T(8,128)(2,1)}, bf16[64,4096]{1,0:T(8,128)(2,1)}, u32[]{:S(2)}, u32[]{:S(2)}) collective-permute-start(bf16[64,4096]{1,0:T(8,128)(2,1)} %fusion.4), channel_id=1, source_target_pairs={{0,7},{1,0},{2,1},{3,2},{4,3},{5,4},{6,5},{7,6},{8,15},{9,8},{10,9... | collective-permute-start | bytes 1572872 | tf_op jit(solution)/shard_map/ppermute | solution.py:70
  260.2 26.0 %all-to-all-start.3 = ((bf16[8,24,4096]{2,1,0:T(8,128)(2,1)}), bf16[8,24,4096]{2,1,0:T(8,128)(2,1)}, u32[]{:S(2)}, u32[]{:S(2)}) async-start(bf16[8,24,4096]{2,1,0:T(8,128)(2,1)} %bitcast.12), calls=%async_computation.3 | async-start | bytes 3145728 | tf_op jit(solution)/shard_map/all_to_all | solution.py:62
  280.6 14.9 %collective-permute-start.18 = (bf16[64,4096]{1,0:T(8,128)(2,1)}, bf16[64,4096]{1,0:T(8,128)(2,1)}, u32[]{:S(2)}, u32[]{:S(2)}) collective-permute-start(bf16[64,4096]{1,0:T(8,128)(2,1)} %fusion.3), channel_id=1, source_target_pairs={{0,7},{1,0},{2,1},{3,2},{4,3},{5,4},{6,5},{7,6},{8,15},{9,8},{10,9... | collective-permute-start | bytes 1572872 | tf_op jit(solution)/shard_map/ppermute | solution.py:70
  284.2 20.4 %collective-permute-start.24 = (bf16[512,768]{1,0:T(8,128)(2,1)S(1)}, bf16[512,768]{1,0:T(8,128)(2,1)S(1)}, u32[]{:S(2)}, u32[]{:S(2)}) collective-permute-start(bf16[512,768]{1,0:T(8,128)(2,1)S(1)} %get-tuple-element.30), channel_id=1, source_target_pairs={{0,128},{128,0},{1,129},{129,1},{2,130},{130,2},{3,131},{131,3},{4... | collective-permute-start | bytes 2359304 | tf_op jit(solution)/shard_map/ppermute | solution.py:66
  284.2 37.3 %collective-permute-start.26 = (bf16[512,768]{1,0:T(8,128)(2,1)}, bf16[512,768]{1,0:T(8,128)(2,1)S(1)}, u32[]{:S(2)}, u32[]{:S(2)}) collective-permute-start(bf16[512,768]{1,0:T(8,128)(2,1)} %get-tuple-element.31), channel_id=1, source_target_pairs={{0,128},{128,0},{1,129},{129,1},{2,130},{130,2},{3,131},{131,3},{4... | collective-permute-start | bytes 2359304 | tf_op jit(solution)/shard_map/ppermute | solution.py:66
  293.3 36.4 %collective-permute-start.22 = (bf16[64,4096]{1,0:T(8,128)(2,1)}, bf16[64,4096]{1,0:T(8,128)(2,1)}, u32[]{:S(2)}, u32[]{:S(2)}) collective-permute-start(bf16[64,4096]{1,0:T(8,128)(2,1)} %fusion.5), channel_id=1, source_target_pairs={{0,1},{1,2},{2,3},{3,4},{4,5},{5,6},{6,7},{7,0},{8,9},{9,10},{10,1... | collective-permute-start | bytes 1572872 | tf_op jit(solution)/shard_map/ppermute | solution.py:70
  298.2 31.4 %collective-permute-start.19 = (bf16[64,4096]{1,0:T(8,128)(2,1)}, bf16[64,4096]{1,0:T(8,128)(2,1)}, u32[]{:S(2)}, u32[]{:S(2)}) collective-permute-start(bf16[64,4096]{1,0:T(8,128)(2,1)} %fusion.2), channel_id=1, source_target_pairs={{0,7},{1,0},{2,1},{3,2},{4,3},{5,4},{6,5},{7,6},{8,15},{9,8},{10,9... | collective-permute-start | bytes 1572872 | tf_op jit(solution)/shard_map/ppermute | solution.py:70
  309.5 31.0 %collective-permute-start.25 = (bf16[512,768]{1,0:T(8,128)(2,1)}, bf16[512,768]{1,0:T(8,128)(2,1)S(1)}, u32[]{:S(2)}, u32[]{:S(2)}) collective-permute-start(bf16[512,768]{1,0:T(8,128)(2,1)} %adam.2), channel_id=1, source_target_pairs={{0,32},{32,0},{1,33},{33,1},{2,34},{34,2},{3,35},{35,3},{4,36},{36... | collective-permute-start | bytes 2359304 | tf_op jit(solution)/shard_map/ppermute | solution.py:66
  326.3 29.2 %collective-permute-start.27 = (bf16[512,768]{1,0:T(8,128)(2,1)}, bf16[512,768]{1,0:T(8,128)(2,1)S(1)}, u32[]{:S(2)}, u32[]{:S(2)}) collective-permute-start(bf16[512,768]{1,0:T(8,128)(2,1)} %adam.3), channel_id=1, source_target_pairs={{0,32},{32,0},{1,33},{33,1},{2,34},{34,2},{3,35},{35,3},{4,36},{36... | collective-permute-start | bytes 2359304 | tf_op jit(solution)/shard_map/ppermute | solution.py:66
  (48 other events, 445.0 us)

commit v2 on v1

--- a/solution.py
+++ b/solution.py
@@ -13,7 +13,7 @@
 LANES = 8
 GROUPS = ((-1, 1), (-2, 2), (-4, 3, -3, 0))
 BACK = ((1, 0), (2, 0), (2, 1), (0, 0))
-SWAP_PARTS = 2
+SWAP_PARTS = (5, 3)
 
 
 def adam_kernel(a, b, c, first, second, out):
@@ -31,10 +31,10 @@
     lax.fori_loop(0, out.shape[0] // bn, rows, 0)
 
 
-def adam_direction(own, from_core, from_x, first, second, part):
+def adam_direction(own, from_core, from_x, first, second, start):
     rows, hidden = from_x.shape
-    bn = 256
-    skip = part * (rows // bn)
+    bn = 128
+    skip = start // bn
     long = pl.BlockSpec((1, bn, hidden), lambda i: (0, i + skip, 0))
     short = pl.BlockSpec((bn, hidden), lambda i: (i, 0))
     return pl.pallas_call(
@@ -313,12 +313,13 @@
     kept = weight_grad(me_ref, xs, grad_rows, 0)
     other = (kept[1].astype(f32) + from_core[1].astype(f32)).astype(bf16)
     moving = jnp.sum(jnp.where(jnp.arange(slots, dtype=i32) == here, swap_mask, 0)) == 1
-    size = shard // SWAP_PARTS
     steps = []
-    for s in range(SWAP_PARTS):
-        at = slice(s * size, (s + 1) * size)
+    start = 0
+    for eighths in SWAP_PARTS:
+        at = slice(start, start + shard // 8 * eighths)
         from_x = swapped(other[at], "xl")
-        stepped = adam_direction(kept, from_core, from_x, first_moment, second_moment, s)
+        stepped = adam_direction(kept, from_core, from_x, first_moment, second_moment, start)
+        start = at.stop
         partner = swapped(stepped, "xh")
         steps.append(jnp.where(moving, partner, stepped))
     adam_step = jnp.concatenate(steps, axis=0)[None]

time: 362 us -> 360 us (level)
  blocking collectives: 0 us -> 27.6 us
  waiting for transfers between devices: 134 us -> 110 us
  starting transfers between devices: 89.7 us -> 84.9 us
  local copies, waits for them, and re-layouts: 28.7 us -> 25 us
    all_to_all x0 -> x1, blocking collectives: none -> 27.6 us  [exchange_plane(): lax.all_to_all(block, ('xl', 'xh', 'y'), 0, 0, axis_index_groups=groups,...]
    ppermute x21, waiting for transfers between devices: 64.3 us -> 52.6 us  [shifted(): lax.ppermute(block, 'z', [(i, (i + by) % PLANES) for i in range(PLANES)])]
    ppermute x7, waiting for transfers between devices: 39.3 us -> 30 us  [swapped(): return lax.ppermute(block, axis, [(0, 1), (1, 0)])]
    all_to_all x7 -> x6, starting transfers between devices: 44.1 us -> 39.4 us  [exchange_plane(): lax.all_to_all(block, ('xl', 'xh', 'y'), 0, 0, axis_index_groups=groups,...]
    all_to_all x7 -> x6, waiting for transfers between devices: 30.5 us -> 27.3 us  [exchange_plane(): lax.all_to_all(block, ('xl', 'xh', 'y'), 0, 0, axis_index_groups=groups,...]
    unnamed x77 -> x75, local copies, waits for them, and re-layouts: 12.4 us -> 11.5 us
  transfers between devices with their start and end apart: 35 -> 34, of which waited for: 17 -> 15; matrix products, arithmetic and copies ran while one was open for 13% -> 12% of each run, Pallas kernels for 19% -> 19%
where the time goes in v2:
time: 360 us; the launch traced here: 355 us
  waiting for transfers between devices  110 us (31%)
  starting transfers between devices  84.9 us (24%)
  Pallas kernels  73.5 us (20%)
  blocking collectives  27.6 us (8%)
  local copies, waits for them, and re-layouts  25 us (7%)
  matrix products  19.6 us (5%)
  other arithmetic  13 us (4%)
    ppermute x21, waiting for transfers between devices, shifted(): lax.ppermute(block, 'z', [(i, (i + by) % PLANES) for i in range(PLANES)])  52.6 us
    all_to_all x6, starting transfers between devices, exchange_plane(): lax.all_to_all(block, ('xl', 'xh', 'y'), 0, 0, axis_index_groups=groups,...  39.4 us
    ppermute x21, starting transfers between devices, shifted(): lax.ppermute(block, 'z', [(i, (i + by) % PLANES) for i in range(PLANES)])  38.7 us
    pallas_call x3, Pallas kernels, expert(): pl.pallas_call(functools.partial(expert_kernel, nk), grid=(2, nk), in_spe...  34.3 us
    ppermute x7, waiting for transfers between devices, swapped(): return lax.ppermute(block, axis, [(0, 1), (1, 0)])  30 us
    all_to_all x1, blocking collectives, exchange_plane(): lax.all_to_all(block, ('xl', 'xh', 'y'), 0, 0, axis_index_groups=groups,...  27.6 us
    all_to_all x6, waiting for transfers between devices, exchange_plane(): lax.all_to_all(block, ('xl', 'xh', 'y'), 0, 0, axis_index_groups=groups,...  27.3 us
    dot_general x10, matrix products, dot(): lax.dot_general(a, b, (contract, ((), ())), preferred_element_type=jnp.fl...  19.6 us
  transfers between devices with their start and end apart: 34, of which 15 were waited for; matrix products, arithmetic and copies ran while one was open for 12% of the time, Pallas kernels for 19%

profile of v2, /device:TPU:120, one launch (start us, length us, event | category | flops | bytes accessed | tf_op | source)
XLA Modules:
  0.0 355.0 jit_solution(3630454498308429363)
XLA Ops:
  15.6 7.3 %collective-permute-done.12.refs_6_ = bf16[96,768]{1,0:T(8,128)(2,1)S(1)} collective-permute-done((bf16[96,768]{1,0:T(8,128)(2,1)S(1)}, bf16[96,768]{1,0:T(8,128)(2,1)S(1)}, u32[]{:S(2)}, u32[]{:S(2)}) %collective-permute-start.12) | collective-permute-done | bytes 147488 | tf_op jit(solution)/shard_map/ppermute | solution.py:70
  27.9 4.7 %shard_map.205 = (bf16[192,4864]{1,0:T(8,128)(2,1)}, bf16[192,128]{1,0:T(8,128)(2,1)}) custom-call(bf16[8,128]{1,0:T(8,128)(2,1)} %fusion.30.refs_0_, f32[24,128]{1,0:T(8,128)} %constant.67.clone.refs_1_.refs_2_, f32[24,128]{1,0:T(8,128)} %constant.67.clone.refs_1_.refs_2_, bf16[192,192]{1,0:T(8,128)(2,1)} %fusion.20.refs_3_, bf16[64,4224]{1,0:T(8,128)(2,1)} %copy-done.17, ...), custom_call_target="tpu_custom_call" | custom-call | tf_op jit(solution)/shard_map/pallas_call | solution.py:157
  32.7 7.0 %all-to-all-start.2 = ((bf16[8,24,4864]{2,1,0:T(8,128)(2,1)}), bf16[8,24,4864]{2,1,0:T(8,128)(2,1)S(1)}, u32[]{:S(2)}, u32[]{:S(2)}) async-start(bf16[8,24,4864]{2,1,0:T(8,128)(2,1)} %bitcast.68), calls=%async_computation.2 | async-start | bytes 3735552 | tf_op jit(solution)/shard_map/all_to_all | solution.py:62
  41.7 10.6 %collective-permute-done.1.refs_4_ = bf16[64,4224]{1,0:T(8,128)(2,1)S(1)} collective-permute-done((bf16[64,4224]{1,0:T(8,128)(2,1)}, bf16[64,4224]{1,0:T(8,128)(2,1)S(1)}, u32[]{:S(2)}, u32[]{:S(2)}) %collective-permute-start.1) | collective-permute-done | bytes 540704 | tf_op jit(solution)/shard_map/ppermute | solution.py:70
  54.6 10.1 %collective-permute-done.2.refs_6_ = bf16[64,4224]{1,0:T(8,128)(2,1)S(1)} collective-permute-done((bf16[64,4224]{1,0:T(8,128)(2,1)S(1)}, bf16[64,4224]{1,0:T(8,128)(2,1)S(1)}, u32[]{:S(2)}, u32[]{:S(2)}) %collective-permute-start.2) | collective-permute-done | bytes 540704 | tf_op jit(solution)/shard_map/ppermute | solution.py:70
  70.4 10.3 %collective-permute-done.7.refs_8_ = bf16[96,768]{1,0:T(8,128)(2,1)} collective-permute-done((bf16[96,768]{1,0:T(8,128)(2,1)}, bf16[96,768]{1,0:T(8,128)(2,1)}, u32[]{:S(2)}, u32[]{:S(2)}) %collective-permute-start.7) | collective-permute-done | bytes 147488 | tf_op jit(solution)/shard_map/ppermute | solution.py:70
  80.7 10.5 %collective-permute-start.9 = (bf16[96,768]{1,0:T(8,128)(2,1)}, bf16[96,768]{1,0:T(8,128)(2,1)S(1)}, u32[]{:S(2)}, u32[]{:S(2)}) collective-permute-start(bf16[96,768]{1,0:T(8,128)(2,1)} %get-tuple-element.35), channel_id=1, source_target_pairs={{0,3},{1,4},{2,5},{3,6},{4,7},{5,0},{6,1},{7,2},{8,11},{9,12},{10,... | collective-permute-start | bytes 442376 | tf_op jit(solution)/shard_map/ppermute | solution.py:70
  95.9 6.6 %shard_map.203 = (bf16[384,4864]{1,0:T(8,128)(2,1)}, bf16[192,128]{1,0:T(8,128)(2,1)}, bf16[192,128]{1,0:T(8,128)(2,1)}) custom-call(bf16[8,128]{1,0:T(8,128)(2,1)} %fusion.30.refs_0_, f32[24,128]{1,0:T(8,128)} %constant.67.clone.refs_1_.refs_2_, f32[48,256]{1,0:T(8,128)} %constant.69.clone.refs_2_, bf16[384,384]{1,0:T(8,128)(2,1)} %fusion.16.refs_3_, ...), custom_call_target="tpu_custom_call" | custom-call | tf_op jit(solution)/shard_map/pallas_call | solution.py:157
  103.8 6.9 %all-to-all-start = ((bf16[8,48,4864]{2,1,0:T(8,128)(2,1)}), bf16[8,48,4864]{2,1,0:T(8,128)(2,1)}, u32[]{:S(2)}, u32[]{:S(2)}) async-start(bf16[8,48,4864]{2,1,0:T(8,128)(2,1)} %bitcast.66), calls=%async_computation | async-start | bytes 7471104 | tf_op jit(solution)/shard_map/all_to_all | solution.py:62
  117.0 5.4 %collective-permute-done.14.refs_6_ = bf16[96,768]{1,0:T(8,128)(2,1)S(1)} collective-permute-done((bf16[96,768]{1,0:T(8,128)(2,1)S(1)}, bf16[96,768]{1,0:T(8,128)(2,1)S(1)}, u32[]{:S(2)}, u32[]{:S(2)}) %collective-permute-start.14) | collective-permute-done | bytes 147488 | tf_op jit(solution)/shard_map/ppermute | solution.py:70
  128.5 18.7 %all-to-all-done = bf16[8,48,4864]{2,1,0:T(8,128)(2,1)} async-done(((bf16[8,48,4864]{2,1,0:T(8,128)(2,1)}), bf16[8,48,4864]{2,1,0:T(8,128)(2,1)}, u32[]{:S(2)}, u32[]{:S(2)}) %all-to-all-start) | async-done | bytes 3735584 | tf_op jit(solution)/shard_map/all_to_all | solution.py:62
  147.3 5.3 %all-to-all-start.4 = ((bf16[8,24,4864]{2,1,0:T(8,128)(2,1)}), bf16[8,24,4864]{2,1,0:T(8,128)(2,1)S(1)}, u32[]{:S(2)}, u32[]{:S(2)}) async-start(bf16[8,24,4864]{2,1,0:T(8,128)(2,1)} %bitcast.67), calls=%async_computation.4 | async-start | bytes 3735552 | tf_op jit(solution)/shard_map/all_to_all | solution.py:62
  164.9 12.7 %shard_map.204 = (bf16[384,768]{1,0:T(8,128)(2,1)}, bf16[192,4096]{1,0:T(8,128)(2,1)}, bf16[192,4096]{1,0:T(8,128)(2,1)}) custom-call(bf16[384,4864]{1,0:T(8,128)(2,1)} %bitcast.3.x.g0.g1.g2.refs_2_, bf16[384,4864]{1,0:T(8,128)(2,1)} %bitcast.3.x.g0.g1.g2.refs_2_, bf16[384,4864]{1,0:T(8,128)(2,1)} %bitcast.3.x.g0.g1.g2.refs_2_, ...), custom_call_target="tpu_custom_call" | custom-call | flops 4831838208 | bytes 18874368 | tf_op jit(solution)/shard_map/pallas_call | solution.py:213
  178.9 6.9 %all-to-all-start.6 = ((bf16[8,24,4096]{2,1,0:T(8,128)(2,1)}), bf16[8,24,4096]{2,1,0:T(8,128)(2,1)S(1)}, u32[]{:S(2)}, u32[]{:S(2)}) async-start(bf16[8,24,4096]{2,1,0:T(8,128)(2,1)} %bitcast.72), calls=%async_computation.6 | async-start | bytes 3145728 | tf_op jit(solution)/shard_map/all_to_all | solution.py:62
  185.8 10.8 %shard_map.206 = (bf16[192,768]{1,0:T(8,128)(2,1)}, bf16[192,4096]{1,0:T(8,128)(2,1)}) custom-call(bf16[192,4864]{1,0:T(8,128)(2,1)} %bitcast.49, bf16[192,4864]{1,0:T(8,128)(2,1)} %bitcast.50, bf16[192,4864]{1,0:T(8,128)(2,1)} %bitcast.51, bf16[192,4864]{1,0:T(8,128)(2,1)} %bitcast.52, bf16[4096,768]{1,0:T(8,128)(2,1)} %fusion.7.w), custom_call_target="tpu_custom_call" | custom-call | flops 2415919104 | bytes 15728640 | tf_op jit(solution)/shard_map/pallas_call | solution.py:213
  197.6 10.8 %shard_map.208 = (bf16[192,768]{1,0:T(8,128)(2,1)}, bf16[192,4096]{1,0:T(8,128)(2,1)}) custom-call(bf16[192,4864]{1,0:T(8,128)(2,1)} %bitcast.55, bf16[192,4864]{1,0:T(8,128)(2,1)} %bitcast.56, bf16[192,4864]{1,0:T(8,128)(2,1)} %bitcast.57, bf16[192,4864]{1,0:T(8,128)(2,1)} %bitcast.58, bf16[4096,768]{1,0:T(8,128)(2,1)} %fusion.7.w), custom_call_target="tpu_custom_call" | custom-call | flops 2415919104 | bytes 15728640 | tf_op jit(solution)/shard_map/pallas_call | solution.py:213
  210.4 6.6 %shard_map.210 = bf16[2,1024,768]{2,1,0:T(8,128)(2,1)} custom-call(s32[1]{0:T(128)} %bitcast.20.me, bf16[192,4864]{1,0:T(8,128)(2,1)} %bitcast.53, bf16[192,4864]{1,0:T(8,128)(2,1)} %bitcast.59, bf16[384,4864]{1,0:T(8,128)(2,1)} %bitcast.3.x.g0.g1.g2.refs_2_, bf16[768,768]{1,0:T(8,128)(2,1)} %copy-done.8), custom_call_target="tpu_custom_call" | custom-call | flops 2415919104 | bytes 7471104 | tf_op jit(solution)/shard_map/pallas_call | solution.py:94
  217.0 27.6 %all_to_all.35 = bf16[8,24,4096]{2,1,0:T(8,128)(2,1)S(1)} all-to-all(bf16[8,24,4096]{2,1,0:T(8,128)(2,1)} %bitcast.71), channel_id=1, replica_groups={{0,8,16,24,160,168,176,184},{128,136,144,152,32,40,48,56},{1,9,17,25,16..., dimensions={0} | all-to-all | bytes 3145728 | tf_op jit(solution)/shard_map/all_to_all | solution.py:62
  244.6 6.6 %all-to-all-start.5 = ((bf16[8,24,4096]{2,1,0:T(8,128)(2,1)}), bf16[8,24,4096]{2,1,0:T(8,128)(2,1)}, u32[]{:S(2)}, u32[]{:S(2)}) async-start(bf16[8,24,4096]{2,1,0:T(8,128)(2,1)} %bitcast.70), calls=%async_computation.5 | async-start | bytes 3145728 | tf_op jit(solution)/shard_map/all_to_all | solution.py:62
  257.1 6.6 %shard_map.209.a = bf16[2,1024,768]{2,1,0:T(8,128)(2,1)} custom-call(s32[1]{0:T(128)} %bitcast.20.me, bf16[192,4864]{1,0:T(8,128)(2,1)} %bitcast.54, bf16[192,4864]{1,0:T(8,128)(2,1)} %bitcast.60, bf16[384,4864]{1,0:T(8,128)(2,1)} %bitcast.3.x.g0.g1.g2.refs_2_, bf16[768,768]{1,0:T(8,128)(2,1)} %copy-done.8), custom_call_target="tpu_custom_call" | custom-call | flops 2415919104 | bytes 7471104 | tf_op jit(solution)/shard_map/pallas_call | solution.py:94
  270.2 6.7 %all-to-all-start.3 = ((bf16[8,24,4096]{2,1,0:T(8,128)(2,1)}), bf16[8,24,4096]{2,1,0:T(8,128)(2,1)}, u32[]{:S(2)}, u32[]{:S(2)}) async-start(bf16[8,24,4096]{2,1,0:T(8,128)(2,1)} %bitcast.69), calls=%async_computation.3 | async-start | bytes 3145728 | tf_op jit(solution)/shard_map/all_to_all | solution.py:62
  287.9 8.1 %all-to-all-done.3 = bf16[8,24,4096]{2,1,0:T(8,128)(2,1)} async-done(((bf16[8,24,4096]{2,1,0:T(8,128)(2,1)}), bf16[8,24,4096]{2,1,0:T(8,128)(2,1)}, u32[]{:S(2)}, u32[]{:S(2)}) %all-to-all-start.3) | async-done | bytes 1572896 | tf_op jit(solution)/shard_map/all_to_all | solution.py:62
  309.3 5.9 %adam.2 = bf16[640,768]{1,0:T(8,128)(2,1)} custom-call(bf16[2,1024,768]{2,1,0:T(8,128)(2,1)} %shard_map.209.a, bf16[2,1024,768]{2,1,0:T(8,128)(2,1)} %collective-permute-done.23.b, bf16[640,768]{1,0:T(8,128)(2,1)} %copy-done.12, f32[1,1024,768]{2,1,0:T(8,128)} %first.3, f32[1,1024,768]{2,1,0:T(8,128)} %second.3), custom_call_target="tpu_custom_call" | custom-call | flops 5898240 | bytes 7864320 | tf_op jit(solution)/shard_map/adam/pallas_call | solution.py:40
  331.4 22.2 %collective-permute-done.27 = bf16[384,768]{1,0:T(8,128)(2,1)S(1)} collective-permute-done((bf16[384,768]{1,0:T(8,128)(2,1)}, bf16[384,768]{1,0:T(8,128)(2,1)S(1)}, u32[]{:S(2)}, u32[]{:S(2)}) %collective-permute-start.27) | collective-permute-done | bytes 589856 | tf_op jit(solution)/shard_map/ppermute | solution.py:66
  (165 shorter events, 118.5 us)
Async XLA Ops:
  4.9 21.3 %collective-permute-start = (bf16[64,4224]{1,0:T(8,128)(2,1)S(1)}, bf16[64,4224]{1,0:T(8,128)(2,1)S(1)}, u32[]{:S(2)}, u32[]{:S(2)}) collective-permute-start(bf16[64,4224]{1,0:T(8,128)(2,1)S(1)} %fusion.17.refs_7_), channel_id=1, source_target_pairs={{0,1},{1,2},{2,3},{3,4},{4,5},{5,6},{6,7},{7,0},{8,9},{9,10},{10,1... | collective-permute-start | bytes 1622024 | tf_op jit(solution)/shard_map/ppermute | solution.py:70
  8.2 18.1 %collective-permute-start.4 = (bf16[64,4224]{1,0:T(8,128)(2,1)S(1)}, bf16[64,4224]{1,0:T(8,128)(2,1)S(1)}, u32[]{:S(2)}, u32[]{:S(2)}) collective-permute-start(bf16[64,4224]{1,0:T(8,128)(2,1)S(1)} %fusion.17.refs_7_), channel_id=1, source_target_pairs={{0,7},{1,0},{2,1},{3,2},{4,3},{5,4},{6,5},{7,6},{8,15},{9,8},{10,9... | collective-permute-start | bytes 1622024 | tf_op jit(solution)/shard_map/ppermute | solution.py:70
  32.7 69.8 %all-to-all-start.2 = ((bf16[8,24,4864]{2,1,0:T(8,128)(2,1)}), bf16[8,24,4864]{2,1,0:T(8,128)(2,1)S(1)}, u32[]{:S(2)}, u32[]{:S(2)}) async-start(bf16[8,24,4864]{2,1,0:T(8,128)(2,1)} %bitcast.68), calls=%async_computation.2 | async-start | bytes 3735552 | tf_op jit(solution)/shard_map/all_to_all | solution.py:62
  54.1 56.7 %collective-permute-start.10 = (bf16[1024,768]{1,0:T(8,128)(2,1)S(1)}, bf16[1024,768]{1,0:T(8,128)(2,1)}, u32[]{:S(2)}, u32[]{:S(2)}) collective-permute-start(bf16[1024,768]{1,0:T(8,128)(2,1)S(1)} %bitcast.65), channel_id=1, source_target_pairs={{0,128},{128,0},{1,129},{129,1},{2,130},{130,2},{3,131},{131,3},{4... | collective-permute-start | bytes 4718600 | tf_op jit(solution)/shard_map/ppermute | solution.py:66
  54.3 39.9 %collective-permute-start.6 = (bf16[64,4224]{1,0:T(8,128)(2,1)S(1)}, bf16[64,4224]{1,0:T(8,128)(2,1)S(1)}, u32[]{:S(2)}, u32[]{:S(2)}) collective-permute-start(bf16[64,4224]{1,0:T(8,128)(2,1)S(1)} %collective-permute-done.5.refs_5_), channel_id=1, source_target_pairs={{0,7},{1,0},{2,1},{3,2},{4,3},{5,4},{6,5},{7,6},{8,15},{9,8},{10,9... | collective-permute-start | bytes 1622024 | tf_op jit(solution)/shard_map/ppermute | solution.py:70
  64.7 29.5 %collective-permute-start.3 = (bf16[64,4224]{1,0:T(8,128)(2,1)S(1)}, bf16[64,4224]{1,0:T(8,128)(2,1)S(1)}, u32[]{:S(2)}, u32[]{:S(2)}) collective-permute-start(bf16[64,4224]{1,0:T(8,128)(2,1)S(1)} %collective-permute-done.2.refs_6_), channel_id=1, source_target_pairs={{0,1},{1,2},{2,3},{3,4},{4,5},{5,6},{6,7},{7,0},{8,9},{9,10},{10,1... | collective-permute-start | bytes 1622024 | tf_op jit(solution)/shard_map/ppermute | solution.py:70
  69.2 22.8 %collective-permute-start.8 = (bf16[96,768]{1,0:T(8,128)(2,1)}, bf16[96,768]{1,0:T(8,128)(2,1)S(1)}, u32[]{:S(2)}, u32[]{:S(2)}) collective-permute-start(bf16[96,768]{1,0:T(8,128)(2,1)} %get-tuple-element.36), channel_id=1, source_target_pairs={{0,5},{1,6},{2,7},{3,0},{4,1},{5,2},{6,3},{7,4},{8,13},{9,14},{10,... | collective-permute-start | bytes 442376 | tf_op jit(solution)/shard_map/ppermute | solution.py:70
  103.8 43.4 %all-to-all-start = ((bf16[8,48,4864]{2,1,0:T(8,128)(2,1)}), bf16[8,48,4864]{2,1,0:T(8,128)(2,1)}, u32[]{:S(2)}, u32[]{:S(2)}) async-start(bf16[8,48,4864]{2,1,0:T(8,128)(2,1)} %bitcast.66), calls=%async_computation | async-start | bytes 7471104 | tf_op jit(solution)/shard_map/all_to_all | solution.py:62
  114.1 45.5 %collective-permute-start.11 = (bf16[2,1024,768]{2,1,0:T(8,128)(2,1)}, bf16[2,1024,768]{2,1,0:T(8,128)(2,1)}, u32[]{:S(2)}, u32[]{:S(2)}) collective-permute-start(bf16[2,1024,768]{2,1,0:T(8,128)(2,1)} %pad_maximum_fusion), channel_id=1, source_target_pairs={{0,64},{64,0},{1,65},{65,1},{2,66},{66,2},{3,67},{67,3},{4,68},{68... | collective-permute-start | bytes 9437192 | tf_op jit(solution)/shard_map/ppermute | solution.py:66
  147.3 30.4 %all-to-all-start.4 = ((bf16[8,24,4864]{2,1,0:T(8,128)(2,1)}), bf16[8,24,4864]{2,1,0:T(8,128)(2,1)S(1)}, u32[]{:S(2)}, u32[]{:S(2)}) async-start(bf16[8,24,4864]{2,1,0:T(8,128)(2,1)} %bitcast.67), calls=%async_computation.4 | async-start | bytes 3735552 | tf_op jit(solution)/shard_map/all_to_all | solution.py:62
  178.9 38.1 %all-to-all-start.6 = ((bf16[8,24,4096]{2,1,0:T(8,128)(2,1)}), bf16[8,24,4096]{2,1,0:T(8,128)(2,1)S(1)}, u32[]{:S(2)}, u32[]{:S(2)}) async-start(bf16[8,24,4096]{2,1,0:T(8,128)(2,1)} %bitcast.72), calls=%async_computation.6 | async-start | bytes 3145728 | tf_op jit(solution)/shard_map/all_to_all | solution.py:62
  217.0 64.8 %collective-permute-start.23 = (bf16[2,1024,768]{2,1,0:T(8,128)(2,1)}, bf16[2,1024,768]{2,1,0:T(8,128)(2,1)}, u32[]{:S(2)}, u32[]{:S(2)}) collective-permute-start(bf16[2,1024,768]{2,1,0:T(8,128)(2,1)} %shard_map.210), channel_id=1, source_target_pairs={{0,64},{64,0},{1,65},{65,1},{2,66},{66,2},{3,67},{67,3},{4,68},{68... | collective-permute-start | bytes 9437192 | tf_op jit(solution)/shard_map/ppermute | solution.py:66
  244.6 25.6 %all-to-all-start.5 = ((bf16[8,24,4096]{2,1,0:T(8,128)(2,1)}), bf16[8,24,4096]{2,1,0:T(8,128)(2,1)}, u32[]{:S(2)}, u32[]{:S(2)}) async-start(bf16[8,24,4096]{2,1,0:T(8,128)(2,1)} %bitcast.70), calls=%async_computation.5 | async-start | bytes 3145728 | tf_op jit(solution)/shard_map/all_to_all | solution.py:62
  256.3 20.6 %collective-permute-start.20 = (bf16[64,4096]{1,0:T(8,128)(2,1)}, bf16[64,4096]{1,0:T(8,128)(2,1)}, u32[]{:S(2)}, u32[]{:S(2)}) collective-permute-start(bf16[64,4096]{1,0:T(8,128)(2,1)} %convolution_convert_fusion), channel_id=1, source_target_pairs={{0,1},{1,2},{2,3},{3,4},{4,5},{5,6},{6,7},{7,0},{8,9},{9,10},{10,1... | collective-permute-start | bytes 1572872 | tf_op jit(solution)/shard_map/ppermute | solution.py:70
  268.4 15.3 %collective-permute-start.17 = (bf16[64,4096]{1,0:T(8,128)(2,1)}, bf16[64,4096]{1,0:T(8,128)(2,1)}, u32[]{:S(2)}, u32[]{:S(2)}) collective-permute-start(bf16[64,4096]{1,0:T(8,128)(2,1)} %fusion.4), channel_id=1, source_target_pairs={{0,7},{1,0},{2,1},{3,2},{4,3},{5,4},{6,5},{7,6},{8,15},{9,8},{10,9... | collective-permute-start | bytes 1572872 | tf_op jit(solution)/shard_map/ppermute | solution.py:70
  270.2 25.8 %all-to-all-start.3 = ((bf16[8,24,4096]{2,1,0:T(8,128)(2,1)}), bf16[8,24,4096]{2,1,0:T(8,128)(2,1)}, u32[]{:S(2)}, u32[]{:S(2)}) async-start(bf16[8,24,4096]{2,1,0:T(8,128)(2,1)} %bitcast.69), calls=%async_computation.3 | async-start | bytes 3145728 | tf_op jit(solution)/shard_map/all_to_all | solution.py:62
  279.8 16.3 %collective-permute-start.21 = (bf16[64,4096]{1,0:T(8,128)(2,1)}, bf16[64,4096]{1,0:T(8,128)(2,1)}, u32[]{:S(2)}, u32[]{:S(2)}) collective-permute-start(bf16[64,4096]{1,0:T(8,128)(2,1)} %fusion.6), channel_id=1, source_target_pairs={{0,1},{1,2},{2,3},{3,4},{4,5},{5,6},{6,7},{7,0},{8,9},{9,10},{10,1... | collective-permute-start | bytes 1572872 | tf_op jit(solution)/shard_map/ppermute | solution.py:70
  283.6 24.7 %collective-permute-start.24 = (bf16[640,768]{1,0:T(8,128)(2,1)S(1)}, bf16[640,768]{1,0:T(8,128)(2,1)S(1)}, u32[]{:S(2)}, u32[]{:S(2)}) collective-permute-start(bf16[640,768]{1,0:T(8,128)(2,1)S(1)} %slice_bitcast_fusion.2), channel_id=1, source_target_pairs={{0,128},{128,0},{1,129},{129,1},{2,130},{130,2},{3,131},{131,3},{4... | collective-permute-start | bytes 2949128 | tf_op jit(solution)/shard_map/ppermute | solution.py:66
  285.7 14.8 %collective-permute-start.18 = (bf16[64,4096]{1,0:T(8,128)(2,1)S(1)}, bf16[64,4096]{1,0:T(8,128)(2,1)}, u32[]{:S(2)}, u32[]{:S(2)}) collective-permute-start(bf16[64,4096]{1,0:T(8,128)(2,1)S(1)} %fusion.3), channel_id=1, source_target_pairs={{0,7},{1,0},{2,1},{3,2},{4,3},{5,4},{6,5},{7,6},{8,15},{9,8},{10,9... | collective-permute-start | bytes 1572872 | tf_op jit(solution)/shard_map/ppermute | solution.py:70
  285.9 35.2 %collective-permute-start.26 = (bf16[384,768]{1,0:T(8,128)(2,1)S(1)}, bf16[384,768]{1,0:T(8,128)(2,1)}, u32[]{:S(2)}, u32[]{:S(2)}) collective-permute-start(bf16[384,768]{1,0:T(8,128)(2,1)S(1)} %slice_bitcast_fusion.3), channel_id=1, source_target_pairs={{0,128},{128,0},{1,129},{129,1},{2,130},{130,2},{3,131},{131,3},{4... | collective-permute-start | bytes 1769480 | tf_op jit(solution)/shard_map/ppermute | solution.py:66
  298.8 29.9 %collective-permute-start.22 = (bf16[64,4096]{1,0:T(8,128)(2,1)}, bf16[64,4096]{1,0:T(8,128)(2,1)}, u32[]{:S(2)}, u32[]{:S(2)}) collective-permute-start(bf16[64,4096]{1,0:T(8,128)(2,1)} %fusion.5), channel_id=1, source_target_pairs={{0,1},{1,2},{2,3},{3,4},{4,5},{5,6},{6,7},{7,0},{8,9},{9,10},{10,1... | collective-permute-start | bytes 1572872 | tf_op jit(solution)/shard_map/ppermute | solution.py:70
  303.2 25.5 %collective-permute-start.19 = (bf16[64,4096]{1,0:T(8,128)(2,1)}, bf16[64,4096]{1,0:T(8,128)(2,1)}, u32[]{:S(2)}, u32[]{:S(2)}) collective-permute-start(bf16[64,4096]{1,0:T(8,128)(2,1)} %fusion.2), channel_id=1, source_target_pairs={{0,7},{1,0},{2,1},{3,2},{4,3},{5,4},{6,5},{7,6},{8,15},{9,8},{10,9... | collective-permute-start | bytes 1572872 | tf_op jit(solution)/shard_map/ppermute | solution.py:70
  315.3 38.3 %collective-permute-start.25 = (bf16[640,768]{1,0:T(8,128)(2,1)}, bf16[640,768]{1,0:T(8,128)(2,1)S(1)}, u32[]{:S(2)}, u32[]{:S(2)}) collective-permute-start(bf16[640,768]{1,0:T(8,128)(2,1)} %adam.2), channel_id=1, source_target_pairs={{0,32},{32,0},{1,33},{33,1},{2,34},{34,2},{3,35},{35,3},{4,36},{36... | collective-permute-start | bytes 2949128 | tf_op jit(solution)/shard_map/ppermute | solution.py:66
  325.2 28.3 %collective-permute-start.27 = (bf16[384,768]{1,0:T(8,128)(2,1)}, bf16[384,768]{1,0:T(8,128)(2,1)S(1)}, u32[]{:S(2)}, u32[]{:S(2)}) collective-permute-start(bf16[384,768]{1,0:T(8,128)(2,1)} %adam.3), channel_id=1, source_target_pairs={{0,32},{32,0},{1,33},{33,1},{2,34},{34,2},{3,35},{35,3},{4,36},{36... | collective-permute-start | bytes 1769480 | tf_op jit(solution)/shard_map/ppermute | solution.py:66
  (46 other events, 442.3 us)
